TPU v7x, 256 devices: a whole 4x4x8 slice. The times are simulated.
256 devices in a mesh: expert: 64 (over z, y, core), tensor: 4 (over x).
Axes of the slice: x: 4, y: 4, z: 8, core: 2. Of those that a mesh axis runs over, the one named last changes fastest.
Arguments:
- context: bfloat16 [8192, 4096], P('expert', 'tensor'), may hold values from -6 to 6
- residual_in: bfloat16 [8192, 4096], P('expert')
- out_weight: bfloat16 [4096, 4096], P('tensor', 'expert'), may hold values from -0.09375 to 0.09375
- norm_gain: bfloat16 [4096], replicated, may hold values from 0.099609375 to 1.8984375
- expert_ids: int32 [8192, 8], P('expert'), may hold values from 0 to 63, all different within a row; in each aligned block of 128 rows (0 to 127, 128 to 255, ...) at most 18 rows name the same one
- gate_weights: float32 [8192, 8], P('expert'), may hold values from 0.1 to 1
- gate_matrix: bfloat16 [64, 4096, 1536], P('expert', None, 'tensor'), may hold values from -0.09375 to 0.09375
- lift_matrix: bfloat16 [64, 4096, 1536], P('expert', None, 'tensor'), may hold values from -0.09375 to 0.09375
- down_matrix: bfloat16 [64, 1536, 4096], P('expert', 'tensor'), may hold values from -0.15625 to 0.15625
Outputs:
- layer_out: bfloat16 [8192, 4096], P('expert', 'tensor')
Inputs may be any that keep to these rules, and one draw needn't show every extreme that they name: `expert_ids`: each row names 8 different experts. Within each aligned block of 128 rows (the rows of one index of the expert axis) no expert is named more than 18 times, a bound that some block reaches.
All inputs are finite; a program needn't handle non-finite values.
Results may differ from a plain program's by a relative error of at most 0.009.
Values may be sent and summed in bfloat16 or wider, within the bound.
No kernel may reach another device: no remote copies, remote signals or barrier semaphores. Data moves between devices by JAX's collectives and lax.ppermute only.
A program may use at most 128 MiB of HBM per device.

v0:
```python
import jax
import jax.numpy as jnp
from jax import lax
from jax.sharding import PartitionSpec as P

epsilon = 1e-06


def body(
    context,
    residual_in,
    out_weight,
    norm_gain,
    expert_ids,
    gate_weights,
    gate_matrix,
    lift_matrix,
    down_matrix,
):
    tokens_here, model_width = residual_in.shape
    top_count = expert_ids.shape[1]
    share_width = model_width // lax.axis_size("tensor")
    column_start = lax.axis_index("tensor") * share_width
    experts_all = lax.axis_size("expert") * gate_matrix.shape[0]
    capacity = min(tokens_here, max(2, tokens_here * top_count * 9 // (8 * experts_all)))
    attention_part = jnp.dot(
        context,
        lax.all_gather(out_weight, "expert", axis=1, tiled=True),
        preferred_element_type=jnp.float32,
    )
    attention_out = lax.psum(attention_part, "tensor")
    hidden_state = (residual_in.astype(jnp.float32) + attention_out).astype(jnp.bfloat16)
    widened = hidden_state.astype(jnp.float32)
    squares_mean = jnp.mean(widened * widened, axis=1, keepdims=True)
    normed_full = (
        widened * lax.rsqrt(squares_mean + epsilon) * norm_gain.astype(jnp.float32)
    ).astype(jnp.bfloat16)
    hidden_share = lax.dynamic_slice_in_dim(hidden_state, column_start, share_width, 1)
    flat_ids = expert_ids.reshape(-1)
    onehot_table = (flat_ids[:, None] == jnp.arange(experts_all, dtype=jnp.int32)[None, :]).astype(
        jnp.int32
    )
    earlier = jnp.cumsum(onehot_table, axis=0) - onehot_table
    slot_index = jnp.sum(earlier * onehot_table, axis=1)
    destination = flat_ids * capacity + slot_index
    token_index = jnp.arange(tokens_here * top_count, dtype=jnp.int32) // top_count
    source_width = normed_full.shape[1]
    buffer_rows = jnp.zeros((experts_all * capacity, source_width), jnp.bfloat16)
    buffer_rows = buffer_rows.at[destination].set(normed_full[token_index])
    buffer_rows = buffer_rows.reshape(experts_all, capacity, source_width)
    received = lax.all_to_all(buffer_rows, "expert", split_axis=0, concat_axis=0, tiled=True)
    senders = received.shape[0]
    slots_here = received.shape[1]
    flat_rows = received.reshape(senders * slots_here, model_width)
    gate_values = jnp.dot(flat_rows, gate_matrix[0], preferred_element_type=jnp.float32)
    lift_values = jnp.dot(flat_rows, lift_matrix[0], preferred_element_type=jnp.float32)
    activation = (jax.nn.silu(gate_values) * lift_values).astype(jnp.bfloat16)
    partial_out = jnp.dot(activation, down_matrix[0], preferred_element_type=jnp.float32)
    expert_partial = partial_out.reshape(senders, slots_here, model_width)
    expert_share = lax.psum_scatter(
        expert_partial.astype(jnp.bfloat16), "tensor", scatter_dimension=2, tiled=True
    )
    returned = lax.all_to_all(expert_share, "expert", split_axis=0, concat_axis=0, tiled=True)
    picked = returned.reshape(experts_all * capacity, share_width)[destination]
    picked = picked.reshape(tokens_here, top_count, share_width)
    moe_share = jnp.sum(gate_weights[:, :, None] * picked.astype(jnp.float32), axis=1)
    return (hidden_share.astype(jnp.float32) + moe_share).astype(jnp.bfloat16)


def solution(mesh):
    placed = (
        P("expert", "tensor"),
        P("expert", None),
        P("tensor", "expert"),
        P(),
        P("expert", None),
        P("expert", None),
        P("expert", None, "tensor"),
        P("expert", None, "tensor"),
        P("expert", "tensor", None),
    )
    return jax.shard_map(
        body, mesh=mesh, in_specs=placed, out_specs=P("expert", "tensor"), check_vma=False
    )
```

profile of v0, /device:TPU:1, one launch (start us, length us, event | category | flops | bytes accessed | tf_op | source)
XLA Modules:
  0.0 744.1 jit_solution(13246930377981361659)
XLA Ops:
  6.5 0.0 copy-start
  6.5 0.0 all-gather.2.cloned.1.call-start
  6.5 0.7 all-gather.2.cloned.1.call-update
  7.3 0.0 copy-start.3
  7.3 0.0 all-reduce.2.cloned.1.call-start
  7.3 90.1 %all-gather.2.cloned.1.call-done = bf16[1024,4096]{0,1:T(8,128)(2,1)} async-done(((bf16[1024,64]{0,1:T(8,128)(2,1)}), bf16[1024,4096]{0,1:T(8,128)(2,1)}) %all-gather.2.cloned.1.call-update) | async-done | bytes 8388624 | tf_op jit(solution)/shard_map/all_gather | solution.py:28
  97.4 7.7 %fusion.18 = f32[128,4096]{1,0:T(8,128)} fusion(bf16[128,1024]{1,0:T(8,128)(2,1)} %param.9, bf16[1024,4096]{0,1:T(8,128)(2,1)} %all-gather.2.cloned.1.call-done), kind=kOutput, calls=%fused_computation.40 | convolution fusion | flops 1073741824 | bytes 10747904 | tf_op jit(solution)/shard_map/dot_general | solution.py:26
  105.2 0.0 all-reduce.2.cloned.1.call-update
  105.2 0.0 reduce-scatter.2.cloned.1.call-start
  105.2 0.0 copy-done.3
  105.2 0.1 copy.22
  105.3 0.1 eq.29
  105.4 0.1 eq.25
  105.5 0.7 fusion.17
  106.2 31.1 %reduce-window.6 = s32[64,8,128]{2,1,0:T(8,128)S(1)} reduce-window(s32[64,8,128]{2,1,0:T(8,128)} %fusion.17, s32[]{:T(128)} %constant.17.clone.1), window={size=1x1x128 pad=0_0x0_0x127_0}, to_apply=%region_1.0 | reduce-window | flops 8323072 | bytes 524292 | tf_op jit(solution)/shard_map/reduce-window
  137.4 0.8 slice.12
  138.2 1.1 copy.24
  139.3 0.1 copy.25
  139.4 0.1 copy.21
  139.5 0.1 mul.60
  139.6 0.0 copy-done.4
  139.7 0.1 broadcast_add_fusion
  139.8 0.1 fusion.16
  139.9 26.2 %all-reduce.2.cloned.1.call-done = f32[128,4096]{1,0:T(8,128)} async-done(((f32[128,4096]{1,0:T(8,128)}), f32[128,4096]{1,0:T(8,128)}) %all-reduce.2.cloned.1.call-update) | async-done | bytes 2097168 | tf_op jit(solution)/shard_map/psum | solution.py:31
  166.1 2.3 fusion.10
  168.3 0.0 copy-start.2
  168.3 1.1 copy-done.2
  169.4 1.4 fusion.12
  170.8 16.4 %gather_fusion = bf16[1024,4096]{1,0:T(8,128)(2,1)} fusion(bf16[128,4096]{1,0:T(8,128)(2,1)} %fusion.12, s32[1024]{0:T(1024)S(1)} %broadcast_clamp_fusion.1), kind=kCustom, calls=%fused_computation | custom fusion | bytes 16781312 | tf_op jit(solution)/shard_map/gather | solution.py:49
  187.2 18.2 %scatter_custom_fusion = bf16[1152,4096]{1,0:T(8,128)(2,1)} fusion(s32[1024]{0:T(1024)S(1)} %bitcast.43, bf16[1024,4096]{1,0:T(8,128)(2,1)} %gather_fusion, bf16[]{:T(256)} %constant.38.clone.1), kind=kCustom, calls=%fused_computation.4 | custom fusion | bytes 9437696 | tf_op jit(solution)/shard_map/scatter | solution.py:49
  205.4 13.9 %reshape.114 = bf16[64,18,4096]{2,1,0:T(8,128)(2,1)} reshape(bf16[1152,4096]{1,0:T(8,128)(2,1)} %scatter_custom_fusion) | data formatting | bytes 18874368 | tf_op jit(solution)/shard_map/reshape | solution.py:50
  219.3 285.2 %all_to_all.10 = bf16[64,18,4096]{2,1,0:T(8,128)(2,1)} all-to-all(bf16[64,18,4096]{2,1,0:T(8,128)(2,1)} %reshape.114), channel_id=1, replica_groups=mesh['expert'=64,'tensor'=4] {'expert'}, dimensions={0} | all-to-all | bytes 18874368 | tf_op jit(solution)/shard_map/all_to_all | solution.py:51
  504.5 14.2 %reshape.115 = bf16[1152,4096]{1,0:T(8,128)(2,1)} reshape(bf16[64,18,4096]{2,1,0:T(8,128)(2,1)} %all_to_all.10) | data formatting | bytes 18874368 | tf_op jit(solution)/shard_map/reshape | solution.py:54
  518.7 8.7 %fusion.5 = f32[1152,384]{1,0:T(8,128)S(1)} fusion(bf16[1152,4096]{1,0:T(8,128)(2,1)} %reshape.115, bf16[1,4096,384]{2,1,0:T(8,128)(2,1)} %param.15), kind=kOutput, calls=%fused_computation.11 | convolution fusion | flops 3623878656 | bytes 14352384 | tf_op jit(solution)/shard_map/dot_general | solution.py:55
  527.4 6.2 fusion.7
  533.6 2.2 dot_general.17
  535.8 8.7 %convolution_convert_fusion = bf16[64,18,4096]{2,0,1:T(8,128)(2,1)} fusion(bf16[1,384,4096]{2,1,0:T(8,128)(2,1)S(1)} %copy-done, bf16[64,18,384]{2,1,0:T(8,128)(2,1)} %dot_general.17), kind=kOutput, calls=%fused_computation.3 | convolution fusion | flops 3628597248 | bytes 13467648 | tf_op jit(solution)/shard_map/dot_general | solution.py:58
  544.5 0.0 reduce-scatter.2.cloned.1.call-update
  544.5 87.9 %reduce-scatter.2.cloned.1.call-done = bf16[64,18,1024]{2,0,1:T(8,128)(2,1)} async-done(((bf16[64,18,4096]{2,0,1:T(8,128)(2,1)}), bf16[64,18,1024]{2,0,1:T(8,128)(2,1)}) %reduce-scatter.2.cloned.1.call-update) | async-done | bytes 2359312 | tf_op jit(solution)/shard_map/reduce_scatter | solution.py:60
  632.4 4.7 copy.27
  637.1 10.9 %all-to-all-start.1 = ((bf16[64,18,1024]{2,1,0:T(8,128)(2,1)}), bf16[64,18,1024]{2,1,0:T(8,128)(2,1)}, u32[]{:S(2)}, u32[]{:S(2)}) async-start(bf16[64,18,1024]{2,1,0:T(8,128)(2,1)} %copy.27), calls=%async_computation.2 | async-start | bytes 6291456 | tf_op jit(solution)/shard_map/all_to_all | solution.py:63
  648.1 0.0 copy-done.5
  648.1 0.1 copy.20
  648.2 72.4 %all-to-all-done.1 = bf16[64,18,1024]{2,1,0:T(8,128)(2,1)} async-done(((bf16[64,18,1024]{2,1,0:T(8,128)(2,1)}), bf16[64,18,1024]{2,1,0:T(8,128)(2,1)}, u32[]{:S(2)}, u32[]{:S(2)}) %all-to-all-start.1) | async-done | bytes 2359328 | tf_op jit(solution)/shard_map/all_to_all | solution.py:63
  720.6 4.3 reshape.116
  724.9 8.0 %gather_fusion.1 = bf16[1024,1024]{1,0:T(8,128)(2,1)} fusion(bf16[1152,1024]{1,0:T(8,128)(2,1)} %reshape.116, s32[1024]{0:T(1024)S(1)} %broadcast_clamp_fusion), kind=kCustom, calls=%fused_computation.1 | custom fusion | bytes 4198400 | tf_op jit(solution)/shard_map/gather | solution.py:64
  732.9 2.9 fusion.2
  735.8 1.7 add_convert_fusion.1
  (16 shorter events, 0.1 us)
Async XLA Ops:
  6.5 529.2 %copy-start = (bf16[1,384,4096]{2,1,0:T(8,128)(2,1)S(1)}, bf16[1,384,4096]{2,1,0:T(8,128)(2,1)}, u32[]{:S(2)}) copy-start(bf16[1,384,4096]{2,1,0:T(8,128)(2,1)} %param.17) | copy-start | bytes 9437188
  6.5 90.9 %all-gather.2.cloned.1.call-start = ((), (), s32[]{:S(2)}) async-start(), calls=%async_computation.3 | async-start | bytes 8519680 | tf_op jit(solution)/shard_map/all_gather | solution.py:28
  7.3 98.0 %copy-start.3 = (s32[128,8]{0,1:T(8,128)S(1)}, s32[128,8]{0,1:T(8,128)}, u32[]{:S(2)}) copy-start(s32[128,8]{0,1:T(8,128)} %param.13) | copy-start | bytes 12292
  7.3 158.8 %all-reduce.2.cloned.1.call-start = ((), (), s32[]{:S(2)}) async-start(), calls=%async_computation.4 | async-start | bytes 4194304 | tf_op jit(solution)/shard_map/psum | solution.py:31
  105.2 34.5 %copy-start.4 = (bf16[4096]{0:T(1024)(128)(2,1)S(1)}, bf16[4096]{0:T(1024)(128)(2,1)}, u32[]{:S(2)}) copy-start(bf16[4096]{0:T(1024)(128)(2,1)} %param.12) | copy-start | bytes 24580
  105.2 527.2 %reduce-scatter.2.cloned.1.call-start = ((), (), s32[]{:S(2)}) async-start(), calls=%async_computation.5 | async-start | bytes 11796480 | tf_op jit(solution)/shard_map/reduce_scatter | solution.py:60
  168.3 1.1 copy-start.2
  518.7 8.7 %copy-start.1 = (bf16[1152,4096]{1,0:T(8,128)(2,1)S(1)}, bf16[1152,4096]{1,0:T(8,128)(2,1)}, u32[]{:S(2)}) copy-start(bf16[1152,4096]{1,0:T(8,128)(2,1)} %reshape.115) | copy-start | bytes 28311556
  518.7 8.7 %copy-start.6 = (bf16[1,4096,384]{2,1,0:T(8,128)(2,1)S(1)}, bf16[1,4096,384]{2,1,0:T(8,128)(2,1)}, u32[]{:S(2)}) copy-start(bf16[1,4096,384]{2,1,0:T(8,128)(2,1)} %param.16) | copy-start | bytes 9437188
  637.1 11.0 %copy-start.5 = (f32[128,8]{0,1:T(8,128)S(1)}, f32[128,8]{0,1:T(8,128)}, u32[]{:S(2)}) copy-start(f32[128,8]{0,1:T(8,128)} %param.14) | copy-start | bytes 12292
  637.1 83.4 %all-to-all-start.1 = ((bf16[64,18,1024]{2,1,0:T(8,128)(2,1)}), bf16[64,18,1024]{2,1,0:T(8,128)(2,1)}, u32[]{:S(2)}, u32[]{:S(2)}) async-start(bf16[64,18,1024]{2,1,0:T(8,128)(2,1)} %copy.27), calls=%async_computation.2 | async-start | bytes 6291456 | tf_op jit(solution)/shard_map/all_to_all | solution.py:63
Sparse Core Ops, SparseCore 0:
  10.1 87.2 all-gather.1
  105.3 60.7 all-reduce.1
  544.6 87.7 reduce-scatter.1
where the time goes:
time: 747 us; the launch traced here: 744 us
  blocking collectives  285 us (38%)
  waiting for transfers between devices  277 us (37%)
  local copies, waits for them, and re-layouts  85.7 us (11%)
  other arithmetic  40.4 us (5%)
  matrix products  31.3 us (4%)
  between operations  13.3 us (2%)
  starting transfers between devices  11 us (1%)
    all_to_all x1, blocking collectives, body(): lax.all_to_all(buffer_rows, 'expert', split_axis=0, concat_axis=0, tiled=...  285 us
    all_gather x1, waiting for transfers between devices, body(): lax.all_gather(out_weight, 'expert', axis=1, tiled=True)  90.1 us
    reduce_scatter x1, waiting for transfers between devices, body(): lax.psum_scatter(expert_partial.astype(jnp.bfloat16), 'tensor', scatter_d...  87.9 us
    all_to_all x1, waiting for transfers between devices, body(): lax.all_to_all(expert_share, 'expert', split_axis=0, concat_axis=0, tiled...  72.4 us
    another operation x3, other arithmetic  31.3 us
    psum x1, waiting for transfers between devices, body(): attention_out = lax.psum(attention_part, 'tensor')  26.2 us
    scatter x1, local copies, waits for them, and re-layouts, body(): buffer_rows = buffer_rows.at[destination].set(normed_full[token_index])  18.2 us
    gather x1, local copies, waits for them, and re-layouts, body(): buffer_rows = buffer_rows.at[destination].set(normed_full[token_index])  16.4 us
  transfers between devices with their start and end apart: 4, of which 4 were waited for; matrix products, arithmetic and copies ran while one was open for 5% of the time, Pallas kernels for 0%

commit v1 on v0

v1 whole, which is shorter than its diff:
```python
import functools

import jax
import jax.numpy as jnp
from jax import lax
from jax.experimental import pallas as pl
from jax.experimental.pallas import tpu as pltpu
from jax.sharding import Mesh
from jax.sharding import PartitionSpec as P

epsilon = 1e-06
f32 = jnp.float32
bf16 = jnp.bfloat16
NZ, NY, NC, NX = 8, 4, 2, 4
NE = NZ * NY * NC
ND = NY * NC


def whole(*shape):
    return pl.BlockSpec(shape, lambda *_: (0,) * len(shape))


def params(mib):
    return pltpu.CompilerParams(vmem_limit_bytes=mib << 20)


def route_kernel(ids_ref, gates_ref, table_ref):
    tokens = ids_ref.shape[1]
    experts = lax.broadcasted_iota(jnp.int32, (NE, tokens), 0)
    chosen = jnp.zeros((NE, tokens), f32)
    weight = jnp.zeros((NE, tokens), f32)
    for k in range(ids_ref.shape[0]):
        same = experts == ids_ref[k : k + 1, :]
        chosen = jnp.where(same, 1.0, chosen)
        weight = jnp.where(same, gates_ref[k : k + 1, :], weight)
    rows = lax.broadcasted_iota(jnp.int32, (tokens, tokens), 0)
    columns = lax.broadcasted_iota(jnp.int32, (tokens, tokens), 1)
    before = jnp.where(rows < columns, 1.0, 0.0).astype(bf16)
    rank = jnp.dot(chosen.astype(bf16), before, preferred_element_type=f32)
    slot = jnp.where(chosen > 0.0, rank, -1.0)
    table_ref[:, :ND, :] = slot.reshape(NZ, ND, tokens)
    table_ref[:, ND:, :] = weight.reshape(NZ, ND, tokens)


def positions(table_ref, d, capacity):
    parts = []
    for z in range(NZ):
        slot = table_ref[z, d : d + 1, :]
        parts.append(jnp.where(slot >= 0.0, slot + float(z * capacity), -1.0))
    return jnp.concatenate(parts, axis=1).astype(jnp.int32)


def dispatch_kernel(capacity, table_ref, hidden_ref, out_ref):
    hidden = jnp.concatenate([hidden_ref[z] for z in range(NZ)], axis=1)
    tokens = hidden.shape[0]
    slots = lax.broadcasted_iota(jnp.int32, (NZ * capacity, tokens), 0)
    for d in range(ND):
        pick = jnp.where(slots == positions(table_ref, d, capacity), 1.0, 0.0).astype(bf16)
        out_ref[d] = jnp.dot(pick, hidden, preferred_element_type=f32).astype(bf16)


def combine_kernel(capacity, table_ref, rows_ref, out_ref, total_ref):
    tokens = out_ref.shape[0] * out_ref.shape[1]
    slots = lax.broadcasted_iota(jnp.int32, (NZ * capacity, tokens), 0)
    d = pl.program_id(0)
    parts, gates = [], []
    for z in range(NZ):
        slot = table_ref[z, pl.ds(d, 1), :]
        parts.append(jnp.where(slot >= 0.0, slot + float(z * capacity), -1.0))
        gates.append(table_ref[z, pl.ds(ND + d, 1), :])
    place = jnp.concatenate(parts, axis=1).astype(jnp.int32)
    gate = jnp.concatenate(gates, axis=1)
    spread = jnp.where(slots == place, gate, 0.0)
    high = spread.astype(bf16)
    low = (spread - high.astype(f32)).astype(bf16)
    over = (((0,), (0,)), ((), ()))
    got = rows_ref[0]
    part = lax.dot_general(high, got, over, preferred_element_type=f32)
    part = part + lax.dot_general(low, got, over, preferred_element_type=f32)

    @pl.when(d == 0)
    def _():
        total_ref[...] = part

    @pl.when(d > 0)
    def _():
        total_ref[...] += part

    @pl.when(d == pl.num_programs(0) - 1)
    def _():
        out_ref[...] = total_ref[...].astype(out_ref.dtype).reshape(out_ref.shape)


def up_kernel(width, x_ref, gain_ref, gate_ref, lift_ref, out_ref):
    squares = None
    for q in range(NX):
        h = x_ref[q].astype(f32)
        s = jnp.sum(h * h, axis=1, keepdims=True)
        squares = s if squares is None else squares + s
    scale = lax.rsqrt(squares * (1.0 / width) + epsilon)
    gate = lift = None
    for q in range(NX):
        part = x_ref.shape[2]
        normed = (x_ref[q].astype(f32) * scale * gain_ref[q : q + 1, :]).astype(bf16)
        g = jnp.dot(normed, gate_ref[:, q].reshape(part, -1), preferred_element_type=f32)
        l = jnp.dot(normed, lift_ref[:, q].reshape(part, -1), preferred_element_type=f32)
        gate = g if gate is None else gate + g
        lift = l if lift is None else lift + l
    out_ref[...] = (gate / (1.0 + jnp.exp(-gate)) * lift).astype(bf16)


def down_kernel(act_ref, down_ref, out_ref):
    total = None
    for q in range(NX):
        part = jnp.dot(act_ref[q], down_ref[q], preferred_element_type=f32)
        part = part.astype(bf16).astype(f32)
        total = part if total is None else total + part
    out_ref[...] = total.astype(bf16)


def body(
    context,
    residual_in,
    out_weight,
    norm_gain,
    expert_ids,
    gate_weights,
    gate_matrix,
    lift_matrix,
    down_matrix,
):
    tokens, width = residual_in.shape
    top = expert_ids.shape[1]
    share = width // NX
    piece = share // NZ
    hidden_units = gate_matrix.shape[2]
    capacity = min(tokens, max(2, tokens * top * 9 // (8 * NE)))
    column = NZ * tokens
    rows = ND * NZ * capacity
    x = lax.axis_index("x")

    down_here = down_matrix[0].reshape(hidden_units, NX, share).transpose(1, 0, 2)
    down_here = lax.all_to_all(down_here, "x", split_axis=0, concat_axis=0, tiled=True)

    context_all = lax.all_gather(context, "z", axis=0, tiled=True)
    weight_here = lax.all_gather(out_weight, ("y", "c"), axis=1, tiled=True)
    part = jnp.dot(context_all, weight_here, preferred_element_type=f32)
    attention = lax.psum_scatter(part, "x", scatter_dimension=1, tiled=True)
    residual = lax.dynamic_index_in_dim(
        residual_in.reshape(tokens, NZ, NX, piece), x, 2, keepdims=False
    )
    residual = lax.all_to_all(
        residual.transpose(1, 0, 2), "z", split_axis=0, concat_axis=0, tiled=True
    ).reshape(column, piece)
    hidden_piece = (residual.astype(f32) + attention).astype(bf16)
    hidden_all = lax.all_gather(hidden_piece, "z", axis=0, tiled=False)

    z = lax.axis_index("z")
    own = lax.dynamic_slice_in_dim(hidden_all, z * tokens, tokens, 1)
    own = lax.all_to_all(own, "x", split_axis=0, concat_axis=0, tiled=True)
    own = own.reshape(NX, NZ // NX, tokens, piece).transpose(2, 1, 0, 3).reshape(tokens, share)

    table = pl.pallas_call(
        route_kernel,
        out_shape=jax.ShapeDtypeStruct((NZ, 2 * ND, tokens), f32),
        name="route",
    )(expert_ids.T, gate_weights.T)
    table = lax.all_to_all(table, "z", split_axis=0, concat_axis=0, tiled=True)

    sent = pl.pallas_call(
        functools.partial(dispatch_kernel, capacity),
        out_shape=jax.ShapeDtypeStruct((ND, NZ * capacity, share), bf16),
        compiler_params=params(48),
        name="dispatch",
    )(table, hidden_all)
    received = lax.all_to_all(sent, ("y", "c"), split_axis=0, concat_axis=0, tiled=True)
    gathered = lax.all_gather(received.reshape(rows, share), "x", axis=0, tiled=False)

    block = rows // 4
    gain = norm_gain.astype(f32).reshape(NZ, NX, piece).transpose(1, 0, 2).reshape(NX, share)
    weights = whole(NZ, NX, piece, hidden_units)
    activation = pl.pallas_call(
        functools.partial(up_kernel, width),
        grid=(rows // block,),
        in_specs=[
            pl.BlockSpec((NX, block, share), lambda i: (0, i, 0)),
            whole(NX, share),
            weights,
            weights,
        ],
        out_specs=pl.BlockSpec((block, hidden_units), lambda i: (i, 0)),
        out_shape=jax.ShapeDtypeStruct((rows, hidden_units), bf16),
        compiler_params=params(56),
        name="up",
    )(
        gathered,
        gain,
        gate_matrix.reshape(NZ, NX, piece, hidden_units),
        lift_matrix.reshape(NZ, NX, piece, hidden_units),
    )
    act_all = lax.all_gather(activation, "x", axis=0, tiled=False)
    expert_out = pl.pallas_call(
        down_kernel,
        grid=(rows // block,),
        in_specs=[
            pl.BlockSpec((NX, block, hidden_units), lambda i: (0, i, 0)),
            whole(NX, hidden_units, share),
        ],
        out_specs=pl.BlockSpec((block, share), lambda i: (i, 0)),
        out_shape=jax.ShapeDtypeStruct((rows, share), bf16),
        compiler_params=params(48),
        name="down",
    )(act_all, down_here)
    returned = lax.all_to_all(
        expert_out.reshape(ND, NZ * capacity, share),
        ("y", "c"),
        split_axis=0,
        concat_axis=0,
        tiled=True,
    )
    partial_sum = pl.pallas_call(
        functools.partial(combine_kernel, capacity),
        grid=(ND,),
        in_specs=[
            whole(NZ, 2 * ND, tokens),
            pl.BlockSpec((1, NZ * capacity, share), lambda d: (d, 0, 0)),
        ],
        out_specs=whole(NZ, tokens, share),
        out_shape=jax.ShapeDtypeStruct((NZ, tokens, share), bf16),
        scratch_shapes=[pltpu.VMEM((column, share), f32)],
        compiler_params=params(48),
        name="combine",
    )(table, returned)
    moe = lax.psum_scatter(partial_sum, "z", scatter_dimension=0, tiled=True)
    moe = moe.reshape(tokens, share)
    return (own.astype(f32) + moe.astype(f32)).astype(bf16)


def solution(mesh):
    fine = Mesh(mesh.devices.reshape(NZ, NY, NC, NX), ("z", "y", "c", "x"))
    e = ("z", "y", "c")
    placed = (
        P(e, "x"),
        P(e, None),
        P("x", e),
        P(),
        P(e, None),
        P(e, None),
        P(e, None, "x"),
        P(e, None, "x"),
        P(e, "x", None),
    )
    return jax.shard_map(body, mesh=fine, in_specs=placed, out_specs=P(e, "x"), check_vma=False)
```

time: 747 us -> 488 us (0.65)
  blocking collectives: 285 us -> 176 us
  local copies, waits for them, and re-layouts: 85.7 us -> 12.5 us
  waiting for transfers between devices: 277 us -> 230 us
  Pallas kernels: 0 us -> 42.9 us
  other arithmetic: 40.4 us -> 4.11 us
  matrix products: 31.3 us -> 4.48 us
  starting transfers between devices: 11 us -> 0.25 us
    all_to_all x1 -> x6, blocking collectives: 285 us -> 176 us  [the longest x1 68.6 us: body(): lax.all_to_all(down_here, 'x', split_axis=0, concat_axis=0, tiled=True)]
    all_gather x1 -> x5, waiting for transfers between devices: 90.1 us -> 183 us  [the longest x1 89.9 us: body(): lax.all_gather(received.reshape(rows, share), 'x', axis=0, tiled=False)]
    all_to_all x1 -> x0, waiting for transfers between devices: 72.4 us -> none  [body(): lax.all_to_all(expert_share, 'expert', split_axis=0, concat_axis=0, tiled...]
    pallas_call x0 -> x5, Pallas kernels: none -> 42.9 us  [the longest x1 16.6 us: body(): pl.pallas_call(functools.partial(up_kernel, width), grid=(rows // block,)...]
    reduce_scatter x1 -> x2, waiting for transfers between devices: 87.9 us -> 45.5 us  [the longest x1 26.7 us: body(): moe = lax.psum_scatter(partial_sum, 'z', scatter_dimension=0, tiled=True)]
    reshape x3 -> x1, local copies, waits for them, and re-layouts: 32.5 us -> 0.75 us  [body(): residual_in.reshape(tokens, NZ, NX, piece)]
    another operation x3 -> x0, other arithmetic: 31.3 us -> none
    dot_general x4 -> x1, matrix products: 31.3 us -> 4.48 us  [body(): part = jnp.dot(context_all, weight_here, preferred_element_type=f32)]
  transfers between devices with their start and end apart: 4 -> 7, of which waited for: 4 -> 7; matrix products, arithmetic and copies ran while one was open for 5% -> 2% of each run, Pallas kernels for 0% -> 0%
where the time goes in v1:
time: 488 us; the launch traced here: 484 us
  waiting for transfers between devices  230 us (47%)
  blocking collectives  176 us (36%)
  Pallas kernels  42.9 us (9%)
  between operations  13.6 us (3%)
  local copies, waits for them, and re-layouts  12.5 us (3%)
    all_gather x1, waiting for transfers between devices, body(): lax.all_gather(received.reshape(rows, share), 'x', axis=0, tiled=False)  89.9 us
    all_to_all x1, blocking collectives, body(): lax.all_to_all(down_here, 'x', split_axis=0, concat_axis=0, tiled=True)  68.6 us
    all_gather x1, waiting for transfers between devices, body(): context_all = lax.all_gather(context, 'z', axis=0, tiled=True)  38.7 us
    all_to_all x1, blocking collectives, body(): lax.all_to_all(sent, ('y', 'c'), split_axis=0, concat_axis=0, tiled=True)  38.4 us
    all_to_all x1, blocking collectives, body(): lax.all_to_all(expert_out.reshape(ND, NZ * capacity, share), ('y', 'c'),...  34.1 us
    all_gather x1, waiting for transfers between devices, body(): weight_here = lax.all_gather(out_weight, ('y', 'c'), axis=1, tiled=True)  31.4 us
    reduce_scatter x1, waiting for transfers between devices, body(): moe = lax.psum_scatter(partial_sum, 'z', scatter_dimension=0, tiled=True)  26.7 us
    all_gather x1, waiting for transfers between devices, body(): hidden_all = lax.all_gather(hidden_piece, 'z', axis=0, tiled=False)  21.8 us
  transfers between devices with their start and end apart: 7, of which 7 were waited for; matrix products, arithmetic and copies ran while one was open for 2% of the time, Pallas kernels for 0%

profile of v1, /device:TPU:1, one launch (start us, length us, event | category | flops | bytes accessed | tf_op | source)
XLA Modules:
  0.0 484.1 jit_solution(16950455108693769774)
XLA Ops:
  6.5 0.0 all-gather.10.cloned.1.call-start
  6.5 0.7 all-gather.10.cloned.1.call-update
  7.3 0.0 all-gather.8.cloned.1.call-start
  7.3 0.7 all-gather.8.cloned.1.call-update
  8.0 0.0 reduce-scatter.3.cloned.1.call-start
  8.1 31.4 %all-gather.10.cloned.1.call-done = bf16[1024,512]{0,1:T(8,128)(2,1)} async-done(((bf16[1024,64]{0,1:T(8,128)(2,1)}), bf16[1024,512]{0,1:T(8,128)(2,1)}) %all-gather.10.cloned.1.call-update) | async-done | bytes 1048592 | tf_op jit(solution)/shard_map/all_gather | solution.py:146
  39.4 38.7 %all-gather.8.cloned.1.call-done = bf16[1024,1024]{1,0:T(8,128)(2,1)} async-done(((bf16[128,1024]{1,0:T(8,128)(2,1)}), bf16[1024,1024]{1,0:T(8,128)(2,1)}) %all-gather.8.cloned.1.call-update) | async-done | bytes 2097168 | tf_op jit(solution)/shard_map/all_gather | solution.py:145
  78.1 4.5 fusion.2
  82.6 0.0 reduce-scatter.3.cloned.1.call-update
  82.6 0.0 all-gather.14.cloned.1.call-start
  82.6 1.1 copy-done.1
  83.8 0.7 reshape.33
  84.5 0.5 constant_dynamic-slice_fusion.1
  85.1 0.1 copy.23
  85.2 13.2 %all_to_all.30 = bf16[8,128,128]{2,1,0:T(8,128)(2,1)S(1)} all-to-all(bf16[8,128,128]{2,1,0:T(8,128)(2,1)S(1)} %bitcast.44), channel_id=1, replica_groups=mesh['z'=8,'y'=4,'c'=2,'x'=4] {'z'}, dimensions={0} | all-to-all | bytes 524288 | tf_op jit(solution)/shard_map/all_to_all | solution.py:152
  98.5 18.8 %reduce-scatter.3.cloned.1.call-done = f32[1024,128]{1,0:T(8,128)} async-done(((f32[1024,512]{1,0:T(8,128)}), f32[1024,128]{1,0:T(8,128)}) %reduce-scatter.3.cloned.1.call-update) | async-done | bytes 524304 | tf_op jit(solution)/shard_map/reduce_scatter | solution.py:148
  117.2 1.8 fusion.1
  119.0 0.0 all-gather.14.cloned.1.call-update
  119.1 0.0 all-gather.12.cloned.1.call-start
  119.1 1.5 route.1
  120.6 14.1 %all_to_all.31.table_ref = f32[8,16,128]{2,1,0:T(8,128)S(1)} all-to-all(f32[8,16,128]{2,1,0:T(8,128)} %route.1), channel_id=1, replica_groups=mesh['z'=8,'y'=4,'c'=2,'x'=4] {'z'}, dimensions={0} | all-to-all | bytes 131072 | tf_op jit(solution)/shard_map/all_to_all | solution.py:168
  134.7 21.8 %all-gather.14.cloned.1.call-done = bf16[8192,128]{1,0:T(8,128)(2,1)} async-done(((bf16[1024,128]{1,0:T(8,128)(2,1)}), bf16[8192,128]{1,0:T(8,128)(2,1)}) %all-gather.14.cloned.1.call-update) | async-done | bytes 2097168 | tf_op jit(solution)/shard_map/all_gather | solution.py:156
  156.4 0.0 copy-start
  156.4 1.6 copy-done
  158.0 2.6 dispatch.1
  160.7 38.4 %all_to_all.32 = bf16[8,144,1024]{2,1,0:T(8,128)(2,1)} all-to-all(bf16[8,144,1024]{2,1,0:T(8,128)(2,1)S(1)} %dispatch.1), channel_id=1, replica_groups=mesh['z'=8,'y'=4,'c'=2,'x'=4] {'y','c'}, dimensions={0} | all-to-all | bytes 4718592 | tf_op jit(solution)/shard_map/all_to_all | solution.py:176
  199.1 0.0 all-gather.12.cloned.1.call-update
  199.1 0.0 all-gather.16.cloned.1.call-start
  199.2 0.6 copy-done.2
  199.8 0.6 convert_bitcast_fusion.gain_ref
  200.4 89.9 %all-gather.12.cloned.1.call-done.x_ref = bf16[4,1152,1024]{2,1,0:T(8,128)(2,1)} async-done(((bf16[1,1152,1024]{2,1,0:T(8,128)(2,1)}), bf16[4,1152,1024]{2,1,0:T(8,128)(2,1)}) %all-gather.12.cloned.1.call-update) | async-done | bytes 9437200 | tf_op jit(solution)/shard_map/all_gather | solution.py:177
  290.3 16.6 %up.1 = bf16[1152,384]{1,0:T(8,128)(2,1)} custom-call(bf16[4,1152,1024]{2,1,0:T(8,128)(2,1)} %all-gather.12.cloned.1.call-done.x_ref, f32[4,1024]{1,0:T(4,128)} %convert_bitcast_fusion.gain_ref, bf16[8,4,128,384]{3,2,1,0:T(8,128)(2,1)} %bitcast.41, bf16[8,4,128,384]{3,2,1,0:T(8,128)(2,1)} %bitcast.42), custom_call_target="tpu_custom_call" | custom-call | tf_op jit(solution)/shard_map/up/pallas_call | solution.py:182
  306.9 0.0 all-gather.16.cloned.1.call-update
  306.9 0.0 reduce-scatter.5.cloned.1.call-start
  306.9 3.4 copy.18
  310.4 2.9 copy.19
  313.3 68.6 %all_to_all.33.down_ref = bf16[4,384,1024]{2,1,0:T(8,128)(2,1)S(1)} all-to-all(bf16[4,384,1024]{2,1,0:T(8,128)(2,1)} %bitcast.37), channel_id=1, replica_groups=mesh['z'=8,'y'=4,'c'=2,'x'=4] {'x'}, dimensions={0} | all-to-all | bytes 6291456 | tf_op jit(solution)/shard_map/all_to_all | solution.py:143
  381.9 1.3 all-gather.16.cloned.1.call-done
  383.2 6.9 %down.1 = bf16[1152,1024]{1,0:T(8,128)(2,1)S(1)} custom-call(bf16[4,1152,384]{2,1,0:T(8,128)(2,1)} %bitcast.40, bf16[4,384,1024]{2,1,0:T(8,128)(2,1)S(1)} %all_to_all.33.down_ref), custom_call_target="tpu_custom_call" | custom-call | tf_op jit(solution)/shard_map/down/pallas_call | solution.py:202
  390.1 34.1 %all_to_all.34.rows_ref = bf16[8,144,1024]{2,1,0:T(8,128)(2,1)S(1)} all-to-all(bf16[8,144,1024]{2,1,0:T(8,128)(2,1)S(1)} %bitcast.34), channel_id=1, replica_groups=mesh['z'=8,'y'=4,'c'=2,'x'=4] {'y','c'}, dimensions={0} | all-to-all | bytes 4718592 | tf_op jit(solution)/shard_map/all_to_all | solution.py:214
  424.2 15.3 %combine.1 = bf16[8,128,1024]{2,1,0:T(8,128)(2,1)} custom-call(f32[8,16,128]{2,1,0:T(8,128)S(1)} %all_to_all.31.table_ref, bf16[8,144,1024]{2,1,0:T(8,128)(2,1)S(1)} %all_to_all.34.rows_ref), custom_call_target="tpu_custom_call" | custom-call | tf_op jit(solution)/shard_map/combine/pallas_call | solution.py:221
  439.5 0.0 reduce-scatter.5.cloned.1.call-update
  439.5 1.0 constant_dynamic-slice_fusion
  440.5 7.9 %all_to_all.35 = bf16[8,128,128]{2,1,0:T(8,128)(2,1)S(1)} all-to-all(bf16[8,128,128]{2,1,0:T(8,128)(2,1)S(1)} %constant_dynamic-slice_fusion), channel_id=1, replica_groups=mesh['z'=8,'y'=4,'c'=2,'x'=4] {'x'}, dimensions={0} | all-to-all | bytes 524288 | tf_op jit(solution)/shard_map/all_to_all | solution.py:160
  448.4 0.2 copy.22
  448.6 0.2 reshape.41
  448.8 26.7 %reduce-scatter.5.cloned.1.call-done = bf16[1,128,1024]{2,1,0:T(8,128)(2,1)} async-done(((bf16[8,128,1024]{2,1,0:T(8,128)(2,1)}), bf16[1,128,1024]{2,1,0:T(8,128)(2,1)}) %reduce-scatter.5.cloned.1.call-update) | async-done | bytes 262160 | tf_op jit(solution)/shard_map/reduce_scatter | solution.py:234
  475.5 1.7 fusion
  (2 shorter events, 0.0 us)
Async XLA Ops:
  6.5 32.9 %all-gather.10.cloned.1.call-start = ((), (), s32[]{:S(2)}) async-start(), calls=%async_computation.9 | async-start | bytes 1179648 | tf_op jit(solution)/shard_map/all_gather | solution.py:146
  7.3 70.8 %all-gather.8.cloned.1.call-start = ((), (), s32[]{:S(2)}) async-start(), calls=%async_computation.8 | async-start | bytes 2359296 | tf_op jit(solution)/shard_map/all_gather | solution.py:145
  8.0 109.2 %reduce-scatter.3.cloned.1.call-start = ((), (), s32[]{:S(2)}) async-start(), calls=%async_computation.10 | async-start | bytes 2621440 | tf_op jit(solution)/shard_map/reduce_scatter | solution.py:148
  82.6 1.2 copy-start.1
  82.6 73.9 %all-gather.14.cloned.1.call-start = ((), (), s32[]{:S(2)}) async-start(), calls=%async_computation.13 | async-start | bytes 2359296 | tf_op jit(solution)/shard_map/all_gather | solution.py:156
  119.1 171.2 %all-gather.12.cloned.1.call-start = ((), (), s32[]{:S(2)}) async-start(), calls=%async_computation.11 | async-start | bytes 11796480 | tf_op jit(solution)/shard_map/all_gather | solution.py:177
  156.4 1.6 copy-start
  199.1 0.7 copy-start.2
  199.1 184.1 %all-gather.16.cloned.1.call-start = ((), (), s32[]{:S(2)}) async-start(), calls=%async_computation.14 | async-start | bytes 4423680 | tf_op jit(solution)/shard_map/all_gather | solution.py:201
  306.9 168.6 %reduce-scatter.5.cloned.1.call-start = ((), (), s32[]{:S(2)}) async-start(), calls=%async_computation.12 | async-start | bytes 2359296 | tf_op jit(solution)/shard_map/reduce_scatter | solution.py:234
Sparse Core Ops, SparseCore 0:
  9.2 30.1 all-gather.9
  41.2 36.8 all-gather.7
  82.7 34.4 reduce-scatter.2
  119.2 37.2 all-gather.13
  199.2 90.9 all-gather.11
  307.0 76.1 all-gather.15
  439.6 35.8 reduce-scatter.4

commit v2 on v0

v2 whole, which is shorter than its diff:
```python
import functools

import jax
import jax.numpy as jnp
from jax import lax
from jax.experimental import pallas as pl
from jax.experimental.pallas import tpu as pltpu
from jax.sharding import Mesh
from jax.sharding import PartitionSpec as P

epsilon = 1e-06
f32 = jnp.float32
bf16 = jnp.bfloat16
NZ, NY, NC, NX = 8, 4, 2, 4
NE = NZ * NY * NC
ND = NY * NC
STEPS = (0, 1, 3, 2)
NEAR = (0, 1, -1, 2, -2)
FAR = (3, -3, 4)
TABLE = 32
BY_ROWS = (((0,), (0,)), ((), ()))
BY_COLUMNS = (((1,), (1,)), ((), ()))


def shape(*dims, dtype=bf16):
    return jax.ShapeDtypeStruct(dims, dtype)


def call(kernel, name, outs, *args, scratch=(), mib=32, flops=0, grid=(), specs=None):
    size = sum(a.size * a.dtype.itemsize for a in args)
    blocks = {} if specs is None else dict(grid=grid, in_specs=specs[0], out_specs=specs[1])
    return pl.pallas_call(
        kernel,
        out_shape=outs,
        scratch_shapes=scratch,
        **blocks,
        compiler_params=pltpu.CompilerParams(vmem_limit_bytes=mib << 20),
        cost_estimate=pl.CostEstimate(flops=flops, bytes_accessed=size, transcendentals=0),
        name=name,
    )(*args)


def shift(value, axis, count, step):
    return lax.ppermute(value, axis, [(i, (i + step) % count) for i in range(count)])


def shift_across(value, step):
    pairs = [
        (y * NC + c, ((y + step) % NY) * NC + 1 - c) for y in range(NY) for c in range(NC)
    ]
    return lax.ppermute(value, ("y", "c"), pairs)


def z_ring(value):
    pieces = {0: value}
    right = left = value
    for k in (1, 2, 3):
        right, left = shift(right, "z", NZ, 1), shift(left, "z", NZ, -1)
        pieces[k], pieces[-k] = right, left
    half = value.shape[0] // 2
    pieces[4] = (shift(right[:half], "z", NZ, 1), shift(left[half:], "z", NZ, -1))
    return pieces


def x_ring(value, forward):
    right, left = shift(value, "x", NX, 1), shift(value, "x", NX, -1)
    far = shift(right, "x", NX, 1) if forward else shift(left, "x", NX, -1)
    return value, right, left, far


def route_kernel(ids_ref, gates_ref, residual_ref, out_ref):
    tokens = ids_ref.shape[1]
    piece = out_ref.shape[2]
    x = lax.axis_index("x")
    experts = lax.broadcasted_iota(jnp.int32, (NE, tokens), 0)
    chosen = jnp.zeros((NE, tokens), f32)
    weight = jnp.zeros((NE, tokens), f32)
    for k in range(ids_ref.shape[0]):
        same = experts == ids_ref[k : k + 1, :]
        chosen = jnp.where(same, 1.0, chosen)
        weight = jnp.where(same, gates_ref[k : k + 1, :], weight)
    rows = lax.broadcasted_iota(jnp.int32, (tokens, tokens), 0)
    columns = lax.broadcasted_iota(jnp.int32, (tokens, tokens), 1)
    before = jnp.where(rows < columns, 1.0, 0.0).astype(bf16)
    rank = jnp.dot(chosen.astype(bf16), before, preferred_element_type=f32)
    slot = jnp.where(chosen > 0.0, rank, -1.0)
    high = weight.astype(bf16).astype(f32)
    low = weight - high
    for z in range(NZ):
        column = pl.multiple_of((z * NX + x) * piece, piece)
        out_ref[z, :tokens, :] = residual_ref[:, pl.ds(column, piece)]
        part = [t[z * ND : (z + 1) * ND] for t in (slot, high, low)]
        part.append(jnp.zeros((ND, tokens), f32))
        out_ref[z, tokens:, :] = jnp.concatenate(part, axis=0).astype(bf16)


def project_kernel(count, *refs):
    pieces, weight_ref, outs = refs[:count], refs[count], refs[count + 1 :]
    piece = outs[0].shape[2]
    x = lax.axis_index("x")
    for step, out_ref in zip(STEPS, outs):
        q = lax.rem(x + step, NX)
        weight = weight_ref[pl.ds(pl.multiple_of(q * piece, piece), piece), :]
        block = row = 0
        for ref in pieces:
            part = lax.dot_general(ref[...], weight, BY_COLUMNS, preferred_element_type=f32)
            out_ref[block, row : row + ref.shape[0], :] = part
            row += ref.shape[0]
            if row == out_ref.shape[1]:
                block, row = block + 1, 0


def hidden_kernel(*refs):
    near, far, packed_ref, out_ref = refs[:NX], refs[NX : 2 * NX], refs[2 * NX], refs[2 * NX + 1]
    tokens = out_ref.shape[1]
    z = lax.axis_index("z")
    for group, offsets in ((near, NEAR), (far, FAR)):
        for i, k in enumerate(offsets):
            block = lax.rem(z + NZ - k, NZ)
            total = (group[0][i] + group[1][i]) + (group[2][i] + group[3][i])
            residual = packed_ref[block, :tokens, :].astype(f32)
            out_ref[block] = (residual + total).astype(bf16)


def places(table_ref, d, capacity):
    parts = []
    for z in range(NZ):
        slot = table_ref[z, pl.ds(d, 1), :]
        parts.append(jnp.where(slot >= 0.0, slot + float(z * capacity), -1.0))
    return jnp.concatenate(parts, axis=1).astype(jnp.int32)


def experts_at(step):
    y, c = lax.axis_index("y"), lax.axis_index("c")
    first = lax.rem(y + step, NY) * NC
    return first + c, first + 1 - c


def dispatch_kernel(capacity, packed_ref, *refs):
    pieces = refs[: NZ + 1]
    sent, own = refs[NZ + 1 : NZ + 1 + ND], refs[NZ + 1 + ND : NZ + 1 + ND + NX]
    all_ref, table_ref = refs[-2:]
    tokens = packed_ref.shape[2]
    piece = pieces[0].shape[1]
    x, z = lax.axis_index("x"), lax.axis_index("z")
    row = 0
    for ref, k in zip(pieces, (0, 1, -1, 2, -2, 3, -3, 4, 4)):
        block = lax.rem(z + NZ - k, NZ)
        column = pl.multiple_of(block * piece, piece)
        size = ref.shape[0]
        all_ref[row : row + size, pl.ds(column, piece)] = ref[...]
        row = (row + size) % all_ref.shape[0]
    for i in range(NZ):
        table_ref[i] = packed_ref[i, tokens:, :].astype(f32)
    slots = lax.broadcasted_iota(jnp.int32, (NZ * capacity, NZ * tokens), 0)
    for i, step in enumerate(STEPS):
        for j, d in enumerate(experts_at(step)):
            pick = jnp.where(slots == places(table_ref, d, capacity), 1.0, 0.0).astype(bf16)
            out_ref = sent[NC * i + j]

            @pl.loop(0, all_ref.shape[1] // 256)
            def _(n, pick=pick, out_ref=out_ref):
                span = pl.ds(pl.multiple_of(n * 256, 256), 256)
                rows = jnp.dot(pick, all_ref[:, span], preferred_element_type=f32)
                out_ref[:, span] = rows.astype(bf16)

    mine = pl.ds(pl.multiple_of(z * tokens, tokens), tokens)
    per = NZ // NX
    for ref, step in zip(own, STEPS):
        first = lax.rem(x + step, NX) * per
        for b in range(per):
            ref[b] = all_ref[mine, pl.ds(pl.multiple_of((first + b) * piece, piece), piece)]


def up_kernel(width, *refs):
    pieces, (gain_ref, gate_ref, lift_ref, out_ref, gate_acc, lift_acc) = refs[:NX], refs[NX:]
    share = pieces[0].shape[1]
    x = lax.axis_index("x")
    squares = None
    for ref in pieces:
        h = ref[...].astype(f32)
        s = jnp.sum(h * h, axis=1, keepdims=True)
        squares = s if squares is None else squares + s
    scale = lax.rsqrt(squares * (1.0 / width) + epsilon)
    depth = 2 * gate_ref.shape[2]
    gate_acc[...] = jnp.zeros_like(gate_acc)
    lift_acc[...] = jnp.zeros_like(lift_acc)
    for ref, back in zip(pieces, STEPS):
        q = lax.rem(x + NX - back, NX)

        @pl.loop(0, share // depth)
        def _(k, ref=ref, q=q):
            span = pl.ds(pl.multiple_of(k * depth, depth), depth)
            normed = ref[:, span].astype(f32) * scale * gain_ref[pl.ds(q, 1), span]
            normed = normed.astype(bf16)
            for weight_ref, acc in ((gate_ref, gate_acc), (lift_ref, lift_acc)):
                weight = weight_ref[pl.ds(2 * k, 2), q].reshape(depth, -1)
                acc[...] += jnp.dot(normed, weight, preferred_element_type=f32)

    gate = gate_acc[...]
    out_ref[...] = (gate / (1.0 + jnp.exp(-gate)) * lift_acc[...]).astype(bf16)


def down_kernel(*refs):
    acts, downs, outs = refs[:NX], refs[NX : 2 * NX], refs[2 * NX :]
    total = None
    for act, down in zip(acts, downs):
        part = jnp.dot(act[...], down[...], preferred_element_type=f32)
        part = part.astype(bf16).astype(f32)
        total = part if total is None else total + part
    total = total.astype(bf16)
    rows = outs[0].shape[0]
    for i, out in enumerate(outs):
        out[...] = total[i * rows : (i + 1) * rows]


def combine_kernel(capacity, step, packed_ref, own_ref, other_ref, *refs):
    table_ref, out_ref = refs[-1], refs[-2]
    tokens = packed_ref.shape[2]
    z = pl.program_id(0)
    table_ref[...] = packed_ref[0].astype(f32)
    first = (z * capacity) // 16 * 16
    window = pl.ds(pl.multiple_of(first, 16), 32)
    offset = z * capacity - first
    slots = lax.broadcasted_iota(jnp.int32, (32, tokens), 0) - offset
    slots = slots.astype(f32)
    spread, rows = [], []
    for d, ref in zip(experts_at(step), (own_ref, other_ref)):
        hit = slots == table_ref[pl.ds(d, 1), :]
        hit = hit & (slots >= 0.0)
        for part in (1, 2):
            gate = table_ref[pl.ds(part * ND + d, 1), :]
            spread.append(jnp.where(hit, gate, 0.0))
            rows.append(ref[window, :])
    total = lax.dot_general(
        jnp.concatenate(spread, axis=0).astype(bf16),
        jnp.concatenate(rows, axis=0),
        BY_ROWS,
        preferred_element_type=f32,
    )
    if len(refs) == 3:
        total = total + refs[0][0]
    out_ref[0] = total.astype(out_ref.dtype)


def final_kernel(moe_ref, *refs):
    own, out_ref = refs[:NX], refs[NX]
    piece = own[0].shape[2]
    x = lax.axis_index("x")
    for ref, step in zip(own, STEPS):
        owner = lax.rem(x + NX - step, NX)
        for b in range(ref.shape[0]):
            column = pl.multiple_of((b * NX + owner) * piece, piece)
            total = moe_ref[0, :, pl.ds(column, piece)].astype(f32)
            for i in range(1, NZ):
                total = total + moe_ref[i, :, pl.ds(column, piece)].astype(f32)
            out_ref[:, pl.ds(column, piece)] = (ref[b].astype(f32) + total).astype(bf16)


def body(
    context,
    residual_in,
    out_weight,
    norm_gain,
    expert_ids,
    gate_weights,
    gate_matrix,
    lift_matrix,
    down_matrix,
):
    tokens, width = residual_in.shape
    top = expert_ids.shape[1]
    share = width // NX
    piece = share // NZ
    units = gate_matrix.shape[2]
    capacity = min(tokens, max(2, tokens * top * 9 // (8 * NE)))
    column = NZ * tokens
    slots = NZ * capacity
    x = lax.axis_index("x")

    packed = call(
        route_kernel,
        "route",
        shape(NZ, tokens + TABLE, piece),
        expert_ids.T,
        gate_weights.T,
        residual_in,
    )
    weight = lax.all_gather(out_weight.T, ("y", "c"), axis=0, tiled=True)
    ring = z_ring(context)
    near = call(
        functools.partial(project_kernel, len(NEAR)),
        "project_near",
        [shape(len(NEAR), tokens, piece, dtype=f32)] * NX,
        *[ring[k] for k in NEAR],
        weight,
        flops=2 * len(NEAR) * tokens * share * NX * piece,
    )
    far = call(
        functools.partial(project_kernel, len(FAR) + 1),
        "project_far",
        [shape(len(FAR), tokens, piece, dtype=f32)] * NX,
        *[ring[k] for k in FAR[:-1]],
        *ring[4],
        weight,
        flops=2 * len(FAR) * tokens * share * NX * piece,
    )
    packed, far = lax.optimization_barrier((packed, far))
    packed = lax.all_to_all(packed, "z", split_axis=0, concat_axis=0, tiled=True)
    near = [near[0]] + [shift(p, "x", NX, s) for p, s in zip(near[1:], STEPS[1:])]
    far = [far[0]] + [shift(p, "x", NX, s) for p, s in zip(far[1:], STEPS[1:])]
    hidden = call(
        hidden_kernel, "hidden", shape(NZ, tokens, piece), *near, *far, packed
    ).reshape(column, piece)

    down_here, hidden = lax.optimization_barrier((down_matrix[0], hidden))
    downs = [
        lax.dynamic_slice_in_dim(down_here, lax.rem(x + s, NX) * share, share, 1) for s in STEPS
    ]
    downs = [downs[0]] + [shift(p, "x", NX, s) for p, s in zip(downs[1:], STEPS[1:])]

    ring = z_ring(hidden)
    sent = call(
        functools.partial(dispatch_kernel, capacity),
        "dispatch",
        [shape(slots, share)] * ND + [shape(NZ // NX, tokens, piece)] * NX,
        packed,
        *[ring[k] for k in NEAR],
        *[ring[k] for k in FAR[:-1]],
        *ring[4],
        scratch=[pltpu.VMEM((column, share), bf16), pltpu.VMEM((NZ, TABLE, tokens), f32)],
        flops=2 * ND * slots * column * share,
    )
    sent, downs = lax.optimization_barrier((sent, downs))
    own = sent[ND:]
    own = [own[0]] + [shift(p, "x", NX, s) for p, s in zip(own[1:], STEPS[1:])]

    gain = norm_gain.astype(f32).reshape(NZ, NX, piece).transpose(1, 0, 2).reshape(NX, share)
    gate_here = gate_matrix.reshape(NZ, NX, piece, units)
    lift_here = lift_matrix.reshape(NZ, NX, piece, units)
    total = None
    for i, step in enumerate(STEPS):
        near_rows, far_rows = sent[NC * i : NC * i + NC]
        if step:
            near_rows = shift(near_rows, "y", NY, step)
        far_rows = shift_across(far_rows, step)
        rows = jnp.concatenate([near_rows, far_rows], axis=0)
        rows = x_ring(rows, i % 2 == 0)
        act = call(
            functools.partial(up_kernel, width),
            f"up{step}",
            shape(NC * slots, units),
            *rows,
            gain,
            gate_here,
            lift_here,
            scratch=[pltpu.VMEM((NC * slots, units), f32)] * 2,
            flops=4 * NC * slots * width * units,
        )
        acts = x_ring(act, i % 2 == 0)
        back = call(
            down_kernel,
            f"down{step}",
            [shape(slots, share)] * NC,
            *acts,
            *downs,
            flops=2 * NC * slots * NX * units * share,
            grid=(share // 256,),
            specs=(
                [pl.BlockSpec((NC * slots, units), lambda i: (0, 0))] * NX
                + [pl.BlockSpec((units, 256), lambda i: (0, i))] * NX,
                [pl.BlockSpec((slots, 256), lambda i: (0, i))] * NC,
            ),
        )
        near_rows, far_rows = back
        if step:
            near_rows = shift(near_rows, "y", NY, -step)
        far_rows = shift_across(far_rows, -step)
        last = i == len(STEPS) - 1
        block = pl.BlockSpec((1, tokens, share), lambda z: (z, 0, 0))
        rows = pl.BlockSpec((slots, share), lambda z: (0, 0))
        table = pl.BlockSpec((1, TABLE, piece), lambda z: (z, tokens // TABLE, 0))
        total = call(
            functools.partial(combine_kernel, capacity, step),
            f"combine{step}",
            shape(NZ, tokens, share, dtype=bf16 if last else f32),
            packed,
            near_rows,
            far_rows,
            *([] if total is None else [total]),
            scratch=[pltpu.VMEM((TABLE, tokens), f32)],
            flops=4 * NC * NZ * 32 * tokens * share,
            grid=(NZ,),
            specs=([table, rows, rows] + ([] if total is None else [block]), block),
        )
    moe = lax.all_to_all(total, "z", split_axis=0, concat_axis=0, tiled=True)
    return call(final_kernel, "final", shape(tokens, share), moe, *own)


def solution(mesh):
    fine = Mesh(mesh.devices.reshape(NZ, NY, NC, NX), ("z", "y", "c", "x"))
    e = ("z", "y", "c")
    placed = (
        P(e, "x"),
        P(e, None),
        P("x", e),
        P(),
        P(e, None),
        P(e, None),
        P(e, None, "x"),
        P(e, None, "x"),
        P(e, "x", None),
    )
    return jax.shard_map(body, mesh=fine, in_specs=placed, out_specs=P(e, "x"), check_vma=False)
```

time: 747 us -> 367 us (0.49)
  the two profiles are of different devices: /device:TPU:1 before, /device:TPU:6 now
where the time goes in v2:
time: 367 us; the launch traced here: 362 us
  waiting for transfers between devices  182 us (50%)
  starting transfers between devices  99.9 us (27%)
  Pallas kernels  58.7 us (16%)
  between operations  14.1 us (4%)
  local copies, waits for them, and re-layouts  7.42 us (2%)
    ppermute x58, waiting for transfers between devices, shift(): lax.ppermute(value, axis, [(i, (i + step) % count) for i in range(count)])  113 us
    ppermute x58, starting transfers between devices, shift(): lax.ppermute(value, axis, [(i, (i + step) % count) for i in range(count)])  84.7 us
    pallas_call x18, Pallas kernels, call(): pl.pallas_call(kernel, out_shape=outs, scratch_shapes=scratch, **blocks,...  58.7 us
    all_to_all x1, waiting for transfers between devices, body(): moe = lax.all_to_all(total, 'z', split_axis=0, concat_axis=0, tiled=True)  41 us
    ppermute x8, waiting for transfers between devices, shift_across(): return lax.ppermute(value, ('y', 'c'), pairs)  27.5 us
  transfers between devices with their start and end apart: 69, of which 29 were waited for; matrix products, arithmetic and copies ran while one was open for 1% of the time, Pallas kernels for 14%

profile of v2, /device:TPU:6, one launch (start us, length us, event | category | flops | bytes accessed | tf_op | source)
XLA Modules:
  0.0 362.4 jit_solution(2405188816959062162)
XLA Ops:
  9.3 4.0 %collective-permute-start.3 = (bf16[128,1024]{1,0:T(8,128)(2,1)}, bf16[128,1024]{1,0:T(8,128)(2,1)S(1)}, u32[]{:S(2)}, u32[]{:S(2)}) collective-permute-start(bf16[128,1024]{1,0:T(8,128)(2,1)} %refs_0_.1), channel_id=1, source_target_pairs={{0,224},{32,0},{64,32},{96,64},{128,96},{160,128},{192,160},{224,1... | collective-permute-start | bytes 786440 | tf_op jit(solution)/shard_map/ppermute | solution.py:44
  13.3 6.4 %collective-permute-done.refs_1_ = bf16[128,1024]{1,0:T(8,128)(2,1)S(1)} collective-permute-done((bf16[128,1024]{1,0:T(8,128)(2,1)}, bf16[128,1024]{1,0:T(8,128)(2,1)S(1)}, u32[]{:S(2)}, u32[]{:S(2)}) %collective-permute-start) | collective-permute-done | bytes 262176 | tf_op jit(solution)/shard_map/ppermute | solution.py:44
  19.7 3.2 collective-permute-start.4
  22.9 5.5 %collective-permute-done.1.refs_3_ = bf16[128,1024]{1,0:T(8,128)(2,1)S(1)} collective-permute-done((bf16[128,1024]{1,0:T(8,128)(2,1)S(1)}, bf16[128,1024]{1,0:T(8,128)(2,1)S(1)}, u32[]{:S(2)}, u32[]{:S(2)}) %collective-permute-start.1) | collective-permute-done | bytes 262176 | tf_op jit(solution)/shard_map/ppermute | solution.py:44
  28.4 3.2 collective-permute-start.5
  31.7 4.5 %collective-permute-done.2.refs_0_ = bf16[128,1024]{1,0:T(8,128)(2,1)S(1)} collective-permute-done((bf16[128,1024]{1,0:T(8,128)(2,1)S(1)}, bf16[128,1024]{1,0:T(8,128)(2,1)S(1)}, u32[]{:S(2)}, u32[]{:S(2)}) %collective-permute-start.2) | collective-permute-done | bytes 262176 | tf_op jit(solution)/shard_map/ppermute | solution.py:44
  36.3 3.3 collective-permute-start.7
  45.7 5.1 %all-to-all-start = ((bf16[8,160,128]{2,1,0:T(8,128)(2,1)}), bf16[8,160,128]{2,1,0:T(8,128)(2,1)S(1)}, u32[]{:S(2)}, u32[]{:S(2)}) async-start(bf16[8,160,128]{2,1,0:T(8,128)(2,1)} %route.1), calls=%async_computation | async-start | bytes 655360 | tf_op jit(solution)/shard_map/all_to_all | solution.py:309
  56.1 2.4 collective-permute-start.10
  62.1 16.2 %collective-permute-done.12.refs_6_ = f32[3,128,128]{2,1,0:T(8,128)S(1)} collective-permute-done((f32[3,128,128]{2,1,0:T(8,128)S(1)}, f32[3,128,128]{2,1,0:T(8,128)S(1)}, u32[]{:S(2)}, u32[]{:S(2)}) %collective-permute-start.12) | collective-permute-done | bytes 196640 | tf_op jit(solution)/shard_map/ppermute | solution.py:44
  78.5 3.0 collective-permute-start.15
  81.5 6.4 %collective-permute-done.15.refs_2_ = bf16[1024,128]{1,0:T(8,128)(2,1)S(1)} collective-permute-done((bf16[1024,128]{1,0:T(8,128)(2,1)S(1)}, bf16[1024,128]{1,0:T(8,128)(2,1)S(1)}, u32[]{:S(2)}, u32[]{:S(2)}) %collective-permute-start.15) | collective-permute-done | bytes 262176 | tf_op jit(solution)/shard_map/ppermute | solution.py:44
  87.9 3.7 %collective-permute-start.17 = (bf16[1024,128]{1,0:T(8,128)(2,1)S(1)}, bf16[1024,128]{1,0:T(8,128)(2,1)S(1)}, u32[]{:S(2)}, u32[]{:S(2)}) collective-permute-start(bf16[1024,128]{1,0:T(8,128)(2,1)S(1)} %collective-permute-done.15.refs_2_), channel_id=1, source_target_pairs={{0,224},{32,0},{64,32},{96,64},{128,96},{160,128},{192,160},{224,1... | collective-permute-start | bytes 786440 | tf_op jit(solution)/shard_map/ppermute | solution.py:44
  94.7 3.2 collective-permute-start.22
  97.9 3.2 collective-permute-start.19
  101.3 3.8 %collective-permute-done.19.refs_6_ = bf16[1024,128]{1,0:T(8,128)(2,1)S(1)} collective-permute-done((bf16[1024,128]{1,0:T(8,128)(2,1)S(1)}, bf16[1024,128]{1,0:T(8,128)(2,1)S(1)}, u32[]{:S(2)}, u32[]{:S(2)}) %collective-permute-start.19) | collective-permute-done | bytes 262176 | tf_op jit(solution)/shard_map/ppermute | solution.py:44
  105.1 3.8 %collective-permute-start.21 = (bf16[512,128]{1,0:T(8,128)(2,1)S(1)}, bf16[512,128]{1,0:T(8,128)(2,1)S(1)}, u32[]{:S(2)}, u32[]{:S(2)}) collective-permute-start(bf16[512,128]{1,0:T(8,128)(2,1)S(1)} %slice.19), channel_id=1, source_target_pairs={{0,224},{32,0},{64,32},{96,64},{128,96},{160,128},{192,160},{224,1... | collective-permute-start | bytes 393224 | tf_op jit(solution)/shard_map/ppermute | solution.py:44
  109.0 2.4 collective-permute-done.21.refs_8_
  111.4 3.8 %collective-permute-done.20.refs_7_ = bf16[512,128]{1,0:T(8,128)(2,1)S(1)} collective-permute-done((bf16[512,128]{1,0:T(8,128)(2,1)S(1)}, bf16[512,128]{1,0:T(8,128)(2,1)S(1)}, u32[]{:S(2)}, u32[]{:S(2)}) %collective-permute-start.20) | collective-permute-done | bytes 131104 | tf_op jit(solution)/shard_map/ppermute | solution.py:44
  115.1 9.6 %dispatch.1 = (bf16[144,1024]{1,0:T(8,128)(2,1)S(1)}, bf16[144,1024]{1,0:T(8,128)(2,1)S(1)}, bf16[144,1024]{1,0:T(8,128)(2,1)S(1)}, bf16[144,1024]{1,0:T(8,128)(...) custom-call(bf16[8,160,128]{2,1,0:T(8,128)(2,1)S(1)} %all-to-all-don, ...), custom_call_target="tpu_custom_call" | custom-call | flops 2415919104 | bytes 2424832 | tf_op jit(solution)/shard_map/dispatch/pallas_call | solution.py:32
  124.9 11.3 %collective-permute-start.25 = (bf16[144,1024]{1,0:T(8,128)(2,1)S(1)}, bf16[144,1024]{1,0:T(8,128)(2,1)S(1)}, u32[]{:S(2)}, u32[]{:S(2)}) collective-permute-start(bf16[144,1024]{1,0:T(8,128)(2,1)S(1)} %get-tuple-element.83), channel_id=1, source_target_pairs={{0,16},{8,24},{16,0},{24,8},{1,17},{9,25},{17,1},{25,9},{2,18},{10... | collective-permute-start | bytes 884744 | tf_op jit(solution)/shard_map/ppermute | solution.py:44
  139.9 5.4 %collective-permute-done.25 = bf16[144,1024]{1,0:T(8,128)(2,1)S(1)} collective-permute-done((bf16[144,1024]{1,0:T(8,128)(2,1)S(1)}, bf16[144,1024]{1,0:T(8,128)(2,1)S(1)}, u32[]{:S(2)}, u32[]{:S(2)}) %collective-permute-start.25) | collective-permute-done | bytes 294944 | tf_op jit(solution)/shard_map/ppermute | solution.py:44
  145.3 5.5 %collective-permute-done.45 = bf16[144,1024]{1,0:T(8,128)(2,1)S(1)} collective-permute-done((bf16[144,1024]{1,0:T(8,128)(2,1)S(1)}, bf16[144,1024]{1,0:T(8,128)(2,1)S(1)}, u32[]{:S(2)}, u32[]{:S(2)}) %collective-permute-start.45) | collective-permute-done | bytes 294944 | tf_op jit(solution)/shard_map/ppermute | solution.py:44
  150.9 6.1 %collective-permute-done.46 = bf16[144,1024]{1,0:T(8,128)(2,1)S(1)} collective-permute-done((bf16[144,1024]{1,0:T(8,128)(2,1)S(1)}, bf16[144,1024]{1,0:T(8,128)(2,1)S(1)}, u32[]{:S(2)}, u32[]{:S(2)}) %collective-permute-start.46) | collective-permute-done | bytes 294944 | tf_op jit(solution)/shard_map/ppermute | solution.py:51
  159.3 3.3 collective-permute-start.47
  162.7 4.9 %collective-permute-done.26 = bf16[144,1024]{1,0:T(8,128)(2,1)S(1)} collective-permute-done((bf16[144,1024]{1,0:T(8,128)(2,1)S(1)}, bf16[144,1024]{1,0:T(8,128)(2,1)S(1)}, u32[]{:S(2)}, u32[]{:S(2)}) %collective-permute-start.26) | collective-permute-done | bytes 294944 | tf_op jit(solution)/shard_map/ppermute | solution.py:51
  171.1 5.6 %collective-permute-done.48.refs_2_ = bf16[288,1024]{1,0:T(8,128)(2,1)S(1)} collective-permute-done((bf16[288,1024]{1,0:T(8,128)(2,1)S(1)}, bf16[288,1024]{1,0:T(8,128)(2,1)S(1)}, u32[]{:S(2)}, u32[]{:S(2)}) %collective-permute-start.48) | collective-permute-done | bytes 589856 | tf_op jit(solution)/shard_map/ppermute | solution.py:44
  176.7 2.9 collective-permute-done.47.refs_1_
  179.6 12.6 %collective-permute-done.37.refs_1_ = bf16[288,1024]{1,0:T(8,128)(2,1)S(1)} collective-permute-done((bf16[288,1024]{1,0:T(8,128)(2,1)S(1)}, bf16[288,1024]{1,0:T(8,128)(2,1)S(1)}, u32[]{:S(2)}, u32[]{:S(2)}) %collective-permute-start.37) | collective-permute-done | bytes 589856 | tf_op jit(solution)/shard_map/ppermute | solution.py:44
  194.4 10.5 %collective-permute-done.58.refs_3_ = bf16[288,1024]{1,0:T(8,128)(2,1)S(1)} collective-permute-done((bf16[288,1024]{1,0:T(8,128)(2,1)S(1)}, bf16[288,1024]{1,0:T(8,128)(2,1)S(1)}, u32[]{:S(2)}, u32[]{:S(2)}) %collective-permute-start.58) | collective-permute-done | bytes 589856 | tf_op jit(solution)/shard_map/ppermute | solution.py:44
  205.3 5.9 %up0.1.refs_0_ = bf16[288,384]{1,0:T(8,128)(2,1)S(1)} custom-call(bf16[288,1024]{1,0:T(8,128)(2,1)S(1)} %constant_dynamic-update-slice_fusion.6.refs_0_, bf16[288,1024]{1,0:T(8,128)(2,1)S(1)} %collective-permute-done.56.refs_1_, bf16[288,1024]{1,0:T(8,128)(2,1)S(1)} %collective-permute-done.57.refs_2_, ...), custom_call_target="tpu_custom_call" | custom-call | flops 1811939328 | bytes 8667136 | tf_op jit(solution)/shard_map/up0/pallas_call | solution.py:32
  211.2 3.3 collective-permute-start.59
  214.5 5.9 %up1.1.refs_0_ = bf16[288,384]{1,0:T(8,128)(2,1)S(1)} custom-call(bf16[288,1024]{1,0:T(8,128)(2,1)S(1)} %constant_dynamic-update-slice_fusion.4.refs_0_, bf16[288,1024]{1,0:T(8,128)(2,1)S(1)} %collective-permute-done.47.refs_1_, bf16[288,1024]{1,0:T(8,128)(2,1)S(1)} %collective-permute-done.48.refs_2_, ...), custom_call_target="tpu_custom_call" | custom-call | flops 1811939328 | bytes 8667136 | tf_op jit(solution)/shard_map/up1/pallas_call | solution.py:32
  220.8 5.9 %up3.1.refs_0_ = bf16[288,384]{1,0:T(8,128)(2,1)S(1)} custom-call(bf16[288,1024]{1,0:T(8,128)(2,1)S(1)} %constant_dynamic-update-slice_fusion.2.refs_0_, bf16[288,1024]{1,0:T(8,128)(2,1)S(1)} %collective-permute-done.37.refs_1_, bf16[288,1024]{1,0:T(8,128)(2,1)S(1)} %collective-permute-done.38.refs_2_, ...), custom_call_target="tpu_custom_call" | custom-call | flops 1811939328 | bytes 8667136 | tf_op jit(solution)/shard_map/up3/pallas_call | solution.py:32
  226.6 3.5 collective-permute-done.27.refs_1_
  232.3 2.6 collective-permute-done.59.refs_1_
  236.2 5.9 %up2.1.refs_0_ = bf16[288,384]{1,0:T(8,128)(2,1)S(1)} custom-call(bf16[288,1024]{1,0:T(8,128)(2,1)S(1)} %constant_dynamic-update-slice_fusion.refs_0_, bf16[288,1024]{1,0:T(8,128)(2,1)S(1)} %collective-permute-done.27.refs_1_, bf16[288,1024]{1,0:T(8,128)(2,1)S(1)} %collective-permute-done.28.refs_2_, bf16[288,1024]{1,0:T(8,128)(2,1)S(1)} %collective-permute-done.29.refs_3_, ...), custom_call_target="tpu_custom_call" | custom-call | flops 1811939328 | bytes 8667136 | tf_op jit(solution)/shard_map/up2/pallas_call | solution.py:32
  244.6 3.6 %collective-permute-done.61.refs_3_ = bf16[288,384]{1,0:T(8,128)(2,1)S(1)} collective-permute-done((bf16[288,384]{1,0:T(8,128)(2,1)S(1)}, bf16[288,384]{1,0:T(8,128)(2,1)S(1)}, u32[]{:S(2)}, u32[]{:S(2)}) %collective-permute-start.61) | collective-permute-done | bytes 221216 | tf_op jit(solution)/shard_map/ppermute | solution.py:44
  249.7 2.4 down0.1
  254.3 2.4 collective-permute-done.52.refs_3_
  256.7 2.4 down1.1
  261.8 2.4 down3.1
  267.2 2.5 down2.1
  269.7 3.8 %collective-permute-start.33 = (bf16[144,1024]{1,0:T(8,128)(2,1)S(1)}, bf16[144,1024]{1,0:T(8,128)(2,1)S(1)}, u32[]{:S(2)}, u32[]{:S(2)}) collective-permute-start(bf16[144,1024]{1,0:T(8,128)(2,1)S(1)} %get-tuple-element.89), channel_id=1, source_target_pairs={{0,16},{8,24},{16,0},{24,8},{1,17},{9,25},{17,1},{25,9},{2,18},{10... | collective-permute-start | bytes 884744 | tf_op jit(solution)/shard_map/ppermute | solution.py:44
  277.9 16.5 %collective-permute-done.44.other_ref = bf16[144,1024]{1,0:T(8,128)(2,1)S(1)} collective-permute-done((bf16[144,1024]{1,0:T(8,128)(2,1)S(1)}, bf16[144,1024]{1,0:T(8,128)(2,1)S(1)}, u32[]{:S(2)}, u32[]{:S(2)}) %collective-permute-start.44) | collective-permute-done | bytes 294944 | tf_op jit(solution)/shard_map/ppermute | solution.py:51
  296.6 4.2 %combine2.1 = bf16[8,128,1024]{2,1,0:T(8,128)(2,1)} custom-call(bf16[8,160,128]{2,1,0:T(8,128)(2,1)S(1)} %all-to-all-done.refs_8_.packed_ref, bf16[144,1024]{1,0:T(8,128)(2,1)S(1)} %collective-permute-done.33.own_ref, bf16[144,1024]{1,0:T(8,128)(2,1)S(1)} %collective-permute-done.34.other_ref, f32[8,128,1024]{2,1,0:T(8,128)S(1)} %combine3.1.refs_0_), custom_call_target="tpu_custom_call" | custom-call | flops 268435456 | bytes 5111808 | tf_op jit(solution)/shard_map/combine2/pallas_call | solution.py:32
  300.8 4.5 %all-to-all-start.1 = ((bf16[8,128,1024]{2,1,0:T(8,128)(2,1)}), bf16[8,128,1024]{2,1,0:T(8,128)(2,1)S(1)}, u32[]{:S(2)}, u32[]{:S(2)}) async-start(bf16[8,128,1024]{2,1,0:T(8,128)(2,1)} %combine2.1), calls=%async_computation.1 | async-start | bytes 4194304 | tf_op jit(solution)/shard_map/all_to_all | solution.py:396
  313.1 41.0 %all-to-all-done.1.moe_ref = bf16[8,128,1024]{2,1,0:T(8,128)(2,1)S(1)} async-done(((bf16[8,128,1024]{2,1,0:T(8,128)(2,1)}), bf16[8,128,1024]{2,1,0:T(8,128)(2,1)S(1)}, u32[]{:S(2)}, u32[]{:S(2)}) %all-to-all-start.1) | async-done | bytes 2097184 | tf_op jit(solution)/shard_map/all_to_all | solution.py:396
  (141 shorter events, 64.7 us)
Async XLA Ops:
  6.5 36.6 %all-gather.2.cloned.1.call-start = ((), (), s32[]{:S(2)}) async-start(), calls=%async_computation.2 | async-start | bytes 1179648 | tf_op jit(solution)/shard_map/all_gather | solution.py:289
  7.3 12.4 %collective-permute-start = (bf16[128,1024]{1,0:T(8,128)(2,1)}, bf16[128,1024]{1,0:T(8,128)(2,1)S(1)}, u32[]{:S(2)}, u32[]{:S(2)}) collective-permute-start(bf16[128,1024]{1,0:T(8,128)(2,1)} %refs_0_.1), channel_id=1, source_target_pairs={{0,32},{32,64},{64,96},{96,128},{128,160},{160,192},{192,224},{224... | collective-permute-start | bytes 786440 | tf_op jit(solution)/shard_map/ppermute | solution.py:44
  45.7 32.6 %all-to-all-start = ((bf16[8,160,128]{2,1,0:T(8,128)(2,1)}), bf16[8,160,128]{2,1,0:T(8,128)(2,1)S(1)}, u32[]{:S(2)}, u32[]{:S(2)}) async-start(bf16[8,160,128]{2,1,0:T(8,128)(2,1)} %route.1), calls=%async_computation | async-start | bytes 655360 | tf_op jit(solution)/shard_map/all_to_all | solution.py:309
  54.0 24.3 %collective-permute-start.8 = (f32[5,128,128]{2,1,0:T(8,128)S(1)}, f32[5,128,128]{2,1,0:T(8,128)S(1)}, u32[]{:S(2)}, u32[]{:S(2)}) collective-permute-start(f32[5,128,128]{2,1,0:T(8,128)S(1)} %get-tuple-element.62), channel_id=1, source_target_pairs={{0,1},{1,2},{2,3},{3,0},{4,5},{5,6},{6,7},{7,4},{8,9},{9,10},{10,1... | collective-permute-start | bytes 983048 | tf_op jit(solution)/shard_map/ppermute | solution.py:44
  55.6 22.7 %collective-permute-start.9 = (f32[5,128,128]{2,1,0:T(8,128)S(1)}, f32[5,128,128]{2,1,0:T(8,128)S(1)}, u32[]{:S(2)}, u32[]{:S(2)}) collective-permute-start(f32[5,128,128]{2,1,0:T(8,128)S(1)} %get-tuple-element.63), channel_id=1, source_target_pairs={{0,3},{1,0},{2,1},{3,2},{4,7},{5,4},{6,5},{7,6},{8,11},{9,8},{10,9... | collective-permute-start | bytes 983048 | tf_op jit(solution)/shard_map/ppermute | solution.py:44
  56.1 22.2 %collective-permute-start.10 = (f32[5,128,128]{2,1,0:T(8,128)S(1)}, f32[5,128,128]{2,1,0:T(8,128)S(1)}, u32[]{:S(2)}, u32[]{:S(2)}) collective-permute-start(f32[5,128,128]{2,1,0:T(8,128)S(1)} %get-tuple-element.64), channel_id=1, source_target_pairs={{0,2},{1,3},{2,0},{3,1},{4,6},{5,7},{6,4},{7,5},{8,10},{9,11},{10,... | collective-permute-start | bytes 983048 | tf_op jit(solution)/shard_map/ppermute | solution.py:44
  58.6 19.7 %collective-permute-start.12 = (f32[3,128,128]{2,1,0:T(8,128)S(1)}, f32[3,128,128]{2,1,0:T(8,128)S(1)}, u32[]{:S(2)}, u32[]{:S(2)}) collective-permute-start(f32[3,128,128]{2,1,0:T(8,128)S(1)} %get-tuple-element.67), channel_id=1, source_target_pairs={{0,3},{1,0},{2,1},{3,2},{4,7},{5,4},{6,5},{7,6},{8,11},{9,8},{10,9... | collective-permute-start | bytes 589832 | tf_op jit(solution)/shard_map/ppermute | solution.py:44
  59.7 18.6 %collective-permute-start.13 = (f32[3,128,128]{2,1,0:T(8,128)S(1)}, f32[3,128,128]{2,1,0:T(8,128)S(1)}, u32[]{:S(2)}, u32[]{:S(2)}) collective-permute-start(f32[3,128,128]{2,1,0:T(8,128)S(1)} %get-tuple-element.68), channel_id=1, source_target_pairs={{0,2},{1,3},{2,0},{3,1},{4,6},{5,7},{6,4},{7,5},{8,10},{9,11},{10,... | collective-permute-start | bytes 589832 | tf_op jit(solution)/shard_map/ppermute | solution.py:44
  93.9 30.8 %collective-permute-start.24 = (bf16[384,1024]{1,0:T(8,128)(2,1)S(1)}, bf16[384,1024]{1,0:T(8,128)(2,1)S(1)}, u32[]{:S(2)}, u32[]{:S(2)}) collective-permute-start(bf16[384,1024]{1,0:T(8,128)(2,1)S(1)} %get-tuple-element.107), channel_id=1, source_target_pairs={{0,2},{1,3},{2,0},{3,1},{4,6},{5,7},{6,4},{7,5},{8,10},{9,11},{10,... | collective-permute-start | bytes 2359304 | tf_op jit(solution)/shard_map/ppermute | solution.py:44
  94.7 30.1 %collective-permute-start.23 = (bf16[384,1024]{1,0:T(8,128)(2,1)S(1)}, bf16[384,1024]{1,0:T(8,128)(2,1)S(1)}, u32[]{:S(2)}, u32[]{:S(2)}) collective-permute-start(bf16[384,1024]{1,0:T(8,128)(2,1)S(1)} %get-tuple-element.108), channel_id=1, source_target_pairs={{0,3},{1,0},{2,1},{3,2},{4,7},{5,4},{6,5},{7,6},{8,11},{9,8},{10,9... | collective-permute-start | bytes 2359304 | tf_op jit(solution)/shard_map/ppermute | solution.py:44
  94.7 30.1 %collective-permute-start.22 = (bf16[384,1024]{1,0:T(8,128)(2,1)S(1)}, bf16[384,1024]{1,0:T(8,128)(2,1)S(1)}, u32[]{:S(2)}, u32[]{:S(2)}) collective-permute-start(bf16[384,1024]{1,0:T(8,128)(2,1)S(1)} %get-tuple-element.109), channel_id=1, source_target_pairs={{0,1},{1,2},{2,3},{3,0},{4,5},{5,6},{6,7},{7,4},{8,9},{9,10},{10,1... | collective-permute-start | bytes 2359304 | tf_op jit(solution)/shard_map/ppermute | solution.py:44
  124.8 13.8 %collective-permute-start.55 = (bf16[144,1024]{1,0:T(8,128)(2,1)S(1)}, bf16[144,1024]{1,0:T(8,128)(2,1)S(1)}, u32[]{:S(2)}, u32[]{:S(2)}) collective-permute-start(bf16[144,1024]{1,0:T(8,128)(2,1)S(1)} %get-tuple-element.100), channel_id=1, source_target_pairs={{0,4},{4,0},{8,12},{12,8},{16,20},{20,16},{24,28},{28,24},{1,5},{5... | collective-permute-start | bytes 884744 | tf_op jit(solution)/shard_map/ppermute | solution.py:51
  124.9 20.4 %collective-permute-start.25 = (bf16[144,1024]{1,0:T(8,128)(2,1)S(1)}, bf16[144,1024]{1,0:T(8,128)(2,1)S(1)}, u32[]{:S(2)}, u32[]{:S(2)}) collective-permute-start(bf16[144,1024]{1,0:T(8,128)(2,1)S(1)} %get-tuple-element.83), channel_id=1, source_target_pairs={{0,16},{8,24},{16,0},{24,8},{1,17},{9,25},{17,1},{25,9},{2,18},{10... | collective-permute-start | bytes 884744 | tf_op jit(solution)/shard_map/ppermute | solution.py:44
  136.2 23.0 %collective-permute-start.35 = (bf16[144,1024]{1,0:T(8,128)(2,1)S(1)}, bf16[144,1024]{1,0:T(8,128)(2,1)S(1)}, u32[]{:S(2)}, u32[]{:S(2)}) collective-permute-start(bf16[144,1024]{1,0:T(8,128)(2,1)S(1)} %get-tuple-element.91), channel_id=1, source_target_pairs={{0,24},{8,0},{16,8},{24,16},{1,25},{9,1},{17,9},{25,17},{2,26},{10... | collective-permute-start | bytes 884744 | tf_op jit(solution)/shard_map/ppermute | solution.py:44
  137.3 22.0 %collective-permute-start.36 = (bf16[144,1024]{1,0:T(8,128)(2,1)S(1)}, bf16[144,1024]{1,0:T(8,128)(2,1)S(1)}, u32[]{:S(2)}, u32[]{:S(2)}) collective-permute-start(bf16[144,1024]{1,0:T(8,128)(2,1)S(1)} %get-tuple-element.92), channel_id=1, source_target_pairs={{0,28},{4,24},{8,4},{12,0},{16,12},{20,8},{24,20},{28,16},{1,29},{... | collective-permute-start | bytes 884744 | tf_op jit(solution)/shard_map/ppermute | solution.py:51
  137.3 13.4 %collective-permute-start.45 = (bf16[144,1024]{1,0:T(8,128)(2,1)S(1)}, bf16[144,1024]{1,0:T(8,128)(2,1)S(1)}, u32[]{:S(2)}, u32[]{:S(2)}) collective-permute-start(bf16[144,1024]{1,0:T(8,128)(2,1)S(1)} %get-tuple-element.95), channel_id=1, source_target_pairs={{0,8},{8,16},{16,24},{24,0},{1,9},{9,17},{17,25},{25,1},{2,10},{10... | collective-permute-start | bytes 884744 | tf_op jit(solution)/shard_map/ppermute | solution.py:44
  138.6 18.5 %collective-permute-start.46 = (bf16[144,1024]{1,0:T(8,128)(2,1)S(1)}, bf16[144,1024]{1,0:T(8,128)(2,1)S(1)}, u32[]{:S(2)}, u32[]{:S(2)}) collective-permute-start(bf16[144,1024]{1,0:T(8,128)(2,1)S(1)} %get-tuple-element.96), channel_id=1, source_target_pairs={{0,12},{4,8},{8,20},{12,16},{16,28},{20,24},{24,4},{28,0},{1,13},{... | collective-permute-start | bytes 884744 | tf_op jit(solution)/shard_map/ppermute | solution.py:51
  145.2 22.5 %collective-permute-start.57 = (bf16[288,1024]{1,0:T(8,128)(2,1)S(1)}, bf16[288,1024]{1,0:T(8,128)(2,1)S(1)}, u32[]{:S(2)}, u32[]{:S(2)}) collective-permute-start(bf16[288,1024]{1,0:T(8,128)(2,1)S(1)} %constant_dynamic-update-slice_fusion.6.refs_0_), channel_id=1, source_target_pairs={{0,3},{1,0},{2,1},{3,2},{4,7},{5,4},{6,5},{7,6},{8,11},{9,8},{10,9... | collective-permute-start | bytes 1769480 | tf_op jit(solution)/shard_map/ppermute | solution.py:44
  150.8 18.9 %collective-permute-start.56 = (bf16[288,1024]{1,0:T(8,128)(2,1)S(1)}, bf16[288,1024]{1,0:T(8,128)(2,1)S(1)}, u32[]{:S(2)}, u32[]{:S(2)}) collective-permute-start(bf16[288,1024]{1,0:T(8,128)(2,1)S(1)} %constant_dynamic-update-slice_fusion.6.refs_0_), channel_id=1, source_target_pairs={{0,1},{1,2},{2,3},{3,0},{4,5},{5,6},{6,7},{7,4},{8,9},{9,10},{10,1... | collective-permute-start | bytes 1769480 | tf_op jit(solution)/shard_map/ppermute | solution.py:44
  159.2 17.5 %collective-permute-start.48 = (bf16[288,1024]{1,0:T(8,128)(2,1)S(1)}, bf16[288,1024]{1,0:T(8,128)(2,1)S(1)}, u32[]{:S(2)}, u32[]{:S(2)}) collective-permute-start(bf16[288,1024]{1,0:T(8,128)(2,1)S(1)} %constant_dynamic-update-slice_fusion.4.refs_0_), channel_id=1, source_target_pairs={{0,3},{1,0},{2,1},{3,2},{4,7},{5,4},{6,5},{7,6},{8,11},{9,8},{10,9... | collective-permute-start | bytes 1769480 | tf_op jit(solution)/shard_map/ppermute | solution.py:44
  159.3 20.3 %collective-permute-start.47 = (bf16[288,1024]{1,0:T(8,128)(2,1)S(1)}, bf16[288,1024]{1,0:T(8,128)(2,1)S(1)}, u32[]{:S(2)}, u32[]{:S(2)}) collective-permute-start(bf16[288,1024]{1,0:T(8,128)(2,1)S(1)} %constant_dynamic-update-slice_fusion.4.refs_0_), channel_id=1, source_target_pairs={{0,1},{1,2},{2,3},{3,0},{4,5},{5,6},{6,7},{7,4},{8,9},{9,10},{10,1... | collective-permute-start | bytes 1769480 | tf_op jit(solution)/shard_map/ppermute | solution.py:44
  167.5 24.7 %collective-permute-start.37 = (bf16[288,1024]{1,0:T(8,128)(2,1)S(1)}, bf16[288,1024]{1,0:T(8,128)(2,1)S(1)}, u32[]{:S(2)}, u32[]{:S(2)}) collective-permute-start(bf16[288,1024]{1,0:T(8,128)(2,1)S(1)} %constant_dynamic-update-slice_fusion.2.refs_0_), channel_id=1, source_target_pairs={{0,1},{1,2},{2,3},{3,0},{4,5},{5,6},{6,7},{7,4},{8,9},{9,10},{10,1... | collective-permute-start | bytes 1769480 | tf_op jit(solution)/shard_map/ppermute | solution.py:44
  167.8 25.8 %collective-permute-start.28 = (bf16[288,1024]{1,0:T(8,128)(2,1)S(1)}, bf16[288,1024]{1,0:T(8,128)(2,1)S(1)}, u32[]{:S(2)}, u32[]{:S(2)}) collective-permute-start(bf16[288,1024]{1,0:T(8,128)(2,1)S(1)} %constant_dynamic-update-slice_fusion.refs_0_), channel_id=1, source_target_pairs={{0,3},{1,0},{2,1},{3,2},{4,7},{5,4},{6,5},{7,6},{8,11},{9,8},{10,9... | collective-permute-start | bytes 1769480 | tf_op jit(solution)/shard_map/ppermute | solution.py:44
  169.7 35.2 %collective-permute-start.58 = (bf16[288,1024]{1,0:T(8,128)(2,1)S(1)}, bf16[288,1024]{1,0:T(8,128)(2,1)S(1)}, u32[]{:S(2)}, u32[]{:S(2)}) collective-permute-start(bf16[288,1024]{1,0:T(8,128)(2,1)S(1)} %collective-permute-done.56.refs_1_), channel_id=1, source_target_pairs={{0,1},{1,2},{2,3},{3,0},{4,5},{5,6},{6,7},{7,4},{8,9},{9,10},{10,1... | collective-permute-start | bytes 1769480 | tf_op jit(solution)/shard_map/ppermute | solution.py:44
  176.7 34.5 %collective-permute-start.49 = (bf16[288,1024]{1,0:T(8,128)(2,1)S(1)}, bf16[288,1024]{1,0:T(8,128)(2,1)S(1)}, u32[]{:S(2)}, u32[]{:S(2)}) collective-permute-start(bf16[288,1024]{1,0:T(8,128)(2,1)S(1)} %collective-permute-done.48.refs_2_), channel_id=1, source_target_pairs={{0,3},{1,0},{2,1},{3,2},{4,7},{5,4},{6,5},{7,6},{8,11},{9,8},{10,9... | collective-permute-start | bytes 1769480 | tf_op jit(solution)/shard_map/ppermute | solution.py:44
  179.6 40.8 %collective-permute-start.38 = (bf16[288,1024]{1,0:T(8,128)(2,1)S(1)}, bf16[288,1024]{1,0:T(8,128)(2,1)S(1)}, u32[]{:S(2)}, u32[]{:S(2)}) collective-permute-start(bf16[288,1024]{1,0:T(8,128)(2,1)S(1)} %constant_dynamic-update-slice_fusion.2.refs_0_), channel_id=1, source_target_pairs={{0,3},{1,0},{2,1},{3,2},{4,7},{5,4},{6,5},{7,6},{8,11},{9,8},{10,9... | collective-permute-start | bytes 1769480 | tf_op jit(solution)/shard_map/ppermute | solution.py:44
  192.2 28.2 %collective-permute-start.39 = (bf16[288,1024]{1,0:T(8,128)(2,1)S(1)}, bf16[288,1024]{1,0:T(8,128)(2,1)S(1)}, u32[]{:S(2)}, u32[]{:S(2)}) collective-permute-start(bf16[288,1024]{1,0:T(8,128)(2,1)S(1)} %collective-permute-done.37.refs_1_), channel_id=1, source_target_pairs={{0,1},{1,2},{2,3},{3,0},{4,5},{5,6},{6,7},{7,4},{8,9},{9,10},{10,1... | collective-permute-start | bytes 1769480 | tf_op jit(solution)/shard_map/ppermute | solution.py:44
  193.6 36.6 %collective-permute-start.27 = (bf16[288,1024]{1,0:T(8,128)(2,1)S(1)}, bf16[288,1024]{1,0:T(8,128)(2,1)S(1)}, u32[]{:S(2)}, u32[]{:S(2)}) collective-permute-start(bf16[288,1024]{1,0:T(8,128)(2,1)S(1)} %constant_dynamic-update-slice_fusion.refs_0_), channel_id=1, source_target_pairs={{0,1},{1,2},{2,3},{3,0},{4,5},{5,6},{6,7},{7,4},{8,9},{9,10},{10,1... | collective-permute-start | bytes 1769480 | tf_op jit(solution)/shard_map/ppermute | solution.py:44
  204.9 26.6 %collective-permute-start.29 = (bf16[288,1024]{1,0:T(8,128)(2,1)S(1)}, bf16[288,1024]{1,0:T(8,128)(2,1)S(1)}, u32[]{:S(2)}, u32[]{:S(2)}) collective-permute-start(bf16[288,1024]{1,0:T(8,128)(2,1)S(1)} %collective-permute-done.28.refs_2_), channel_id=1, source_target_pairs={{0,3},{1,0},{2,1},{3,2},{4,7},{5,4},{6,5},{7,6},{8,11},{9,8},{10,9... | collective-permute-start | bytes 1769480 | tf_op jit(solution)/shard_map/ppermute | solution.py:44
  211.2 23.7 %collective-permute-start.59 = (bf16[288,384]{1,0:T(8,128)(2,1)S(1)}, bf16[288,384]{1,0:T(8,128)(2,1)S(1)}, u32[]{:S(2)}, u32[]{:S(2)}) collective-permute-start(bf16[288,384]{1,0:T(8,128)(2,1)S(1)} %up0.1.refs_0_), channel_id=1, source_target_pairs={{0,1},{1,2},{2,3},{3,0},{4,5},{5,6},{6,7},{7,4},{8,9},{9,10},{10,1... | collective-permute-start | bytes 663560 | tf_op jit(solution)/shard_map/ppermute | solution.py:44
  220.4 21.7 %collective-permute-start.60 = (bf16[288,384]{1,0:T(8,128)(2,1)S(1)}, bf16[288,384]{1,0:T(8,128)(2,1)S(1)}, u32[]{:S(2)}, u32[]{:S(2)}) collective-permute-start(bf16[288,384]{1,0:T(8,128)(2,1)S(1)} %up0.1.refs_0_), channel_id=1, source_target_pairs={{0,3},{1,0},{2,1},{3,2},{4,7},{5,4},{6,5},{7,6},{8,11},{9,8},{10,9... | collective-permute-start | bytes 663560 | tf_op jit(solution)/shard_map/ppermute | solution.py:44
  220.5 22.6 %collective-permute-start.51 = (bf16[288,384]{1,0:T(8,128)(2,1)S(1)}, bf16[288,384]{1,0:T(8,128)(2,1)S(1)}, u32[]{:S(2)}, u32[]{:S(2)}) collective-permute-start(bf16[288,384]{1,0:T(8,128)(2,1)S(1)} %up1.1.refs_0_), channel_id=1, source_target_pairs={{0,3},{1,0},{2,1},{3,2},{4,7},{5,4},{6,5},{7,6},{8,11},{9,8},{10,9... | collective-permute-start | bytes 663560 | tf_op jit(solution)/shard_map/ppermute | solution.py:44
  230.1 22.0 %collective-permute-start.50 = (bf16[288,384]{1,0:T(8,128)(2,1)S(1)}, bf16[288,384]{1,0:T(8,128)(2,1)S(1)}, u32[]{:S(2)}, u32[]{:S(2)}) collective-permute-start(bf16[288,384]{1,0:T(8,128)(2,1)S(1)} %up1.1.refs_0_), channel_id=1, source_target_pairs={{0,1},{1,2},{2,3},{3,0},{4,5},{5,6},{6,7},{7,4},{8,9},{9,10},{10,1... | collective-permute-start | bytes 663560 | tf_op jit(solution)/shard_map/ppermute | solution.py:44
  231.5 12.9 %collective-permute-start.40 = (bf16[288,384]{1,0:T(8,128)(2,1)S(1)}, bf16[288,384]{1,0:T(8,128)(2,1)S(1)}, u32[]{:S(2)}, u32[]{:S(2)}) collective-permute-start(bf16[288,384]{1,0:T(8,128)(2,1)S(1)} %up3.1.refs_0_), channel_id=1, source_target_pairs={{0,1},{1,2},{2,3},{3,0},{4,5},{5,6},{6,7},{7,4},{8,9},{9,10},{10,1... | collective-permute-start | bytes 663560 | tf_op jit(solution)/shard_map/ppermute | solution.py:44
  234.9 13.3 %collective-permute-start.61 = (bf16[288,384]{1,0:T(8,128)(2,1)S(1)}, bf16[288,384]{1,0:T(8,128)(2,1)S(1)}, u32[]{:S(2)}, u32[]{:S(2)}) collective-permute-start(bf16[288,384]{1,0:T(8,128)(2,1)S(1)} %collective-permute-done.59.refs_1_), channel_id=1, source_target_pairs={{0,1},{1,2},{2,3},{3,0},{4,5},{5,6},{6,7},{7,4},{8,9},{9,10},{10,1... | collective-permute-start | bytes 663560 | tf_op jit(solution)/shard_map/ppermute | solution.py:44
  243.0 13.6 %collective-permute-start.52 = (bf16[288,384]{1,0:T(8,128)(2,1)S(1)}, bf16[288,384]{1,0:T(8,128)(2,1)S(1)}, u32[]{:S(2)}, u32[]{:S(2)}) collective-permute-start(bf16[288,384]{1,0:T(8,128)(2,1)S(1)} %collective-permute-done.51.refs_2_), channel_id=1, source_target_pairs={{0,3},{1,0},{2,1},{3,2},{4,7},{5,4},{6,5},{7,6},{8,11},{9,8},{10,9... | collective-permute-start | bytes 663560 | tf_op jit(solution)/shard_map/ppermute | solution.py:44
  244.4 16.8 %collective-permute-start.41 = (bf16[288,384]{1,0:T(8,128)(2,1)S(1)}, bf16[288,384]{1,0:T(8,128)(2,1)S(1)}, u32[]{:S(2)}, u32[]{:S(2)}) collective-permute-start(bf16[288,384]{1,0:T(8,128)(2,1)S(1)} %up3.1.refs_0_), channel_id=1, source_target_pairs={{0,3},{1,0},{2,1},{3,2},{4,7},{5,4},{6,5},{7,6},{8,11},{9,8},{10,9... | collective-permute-start | bytes 663560 | tf_op jit(solution)/shard_map/ppermute | solution.py:44
  248.2 12.9 %collective-permute-start.42 = (bf16[288,384]{1,0:T(8,128)(2,1)S(1)}, bf16[288,384]{1,0:T(8,128)(2,1)S(1)}, u32[]{:S(2)}, u32[]{:S(2)}) collective-permute-start(bf16[288,384]{1,0:T(8,128)(2,1)S(1)} %collective-permute-done.40.refs_1_), channel_id=1, source_target_pairs={{0,1},{1,2},{2,3},{3,0},{4,5},{5,6},{6,7},{7,4},{8,9},{9,10},{10,1... | collective-permute-start | bytes 663560 | tf_op jit(solution)/shard_map/ppermute | solution.py:44
  252.2 12.1 %collective-permute-start.30 = (bf16[288,384]{1,0:T(8,128)(2,1)S(1)}, bf16[288,384]{1,0:T(8,128)(2,1)S(1)}, u32[]{:S(2)}, u32[]{:S(2)}) collective-permute-start(bf16[288,384]{1,0:T(8,128)(2,1)S(1)} %up2.1.refs_0_), channel_id=1, source_target_pairs={{0,1},{1,2},{2,3},{3,0},{4,5},{5,6},{6,7},{7,4},{8,9},{9,10},{10,1... | collective-permute-start | bytes 663560 | tf_op jit(solution)/shard_map/ppermute | solution.py:44
  253.0 12.8 %collective-permute-start.32 = (bf16[288,384]{1,0:T(8,128)(2,1)S(1)}, bf16[288,384]{1,0:T(8,128)(2,1)S(1)}, u32[]{:S(2)}, u32[]{:S(2)}) collective-permute-start(bf16[288,384]{1,0:T(8,128)(2,1)S(1)} %collective-permute-done.31.refs_2_), channel_id=1, source_target_pairs={{0,3},{1,0},{2,1},{3,2},{4,7},{5,4},{6,5},{7,6},{8,11},{9,8},{10,9... | collective-permute-start | bytes 663560 | tf_op jit(solution)/shard_map/ppermute | solution.py:44
  256.7 13.0 %collective-permute-start.62 = (bf16[144,1024]{1,0:T(8,128)(2,1)S(1)}, bf16[144,1024]{1,0:T(8,128)(2,1)S(1)}, u32[]{:S(2)}, u32[]{:S(2)}) collective-permute-start(bf16[144,1024]{1,0:T(8,128)(2,1)S(1)} %get-tuple-element.102), channel_id=1, source_target_pairs={{0,4},{4,0},{8,12},{12,8},{16,20},{20,16},{24,28},{28,24},{1,5},{5... | collective-permute-start | bytes 884744 | tf_op jit(solution)/shard_map/ppermute | solution.py:51
  261.2 12.3 %collective-permute-start.53 = (bf16[144,1024]{1,0:T(8,128)(2,1)S(1)}, bf16[144,1024]{1,0:T(8,128)(2,1)S(1)}, u32[]{:S(2)}, u32[]{:S(2)}) collective-permute-start(bf16[144,1024]{1,0:T(8,128)(2,1)S(1)} %get-tuple-element.97), channel_id=1, source_target_pairs={{0,24},{8,0},{16,8},{24,16},{1,25},{9,1},{17,9},{25,17},{2,26},{10... | collective-permute-start | bytes 884744 | tf_op jit(solution)/shard_map/ppermute | solution.py:44
  261.2 14.4 %collective-permute-start.54 = (bf16[144,1024]{1,0:T(8,128)(2,1)S(1)}, bf16[144,1024]{1,0:T(8,128)(2,1)S(1)}, u32[]{:S(2)}, u32[]{:S(2)}) collective-permute-start(bf16[144,1024]{1,0:T(8,128)(2,1)S(1)} %get-tuple-element.98), channel_id=1, source_target_pairs={{0,28},{4,24},{8,4},{12,0},{16,12},{20,8},{24,20},{28,16},{1,29},{... | collective-permute-start | bytes 884744 | tf_op jit(solution)/shard_map/ppermute | solution.py:51
  264.3 13.6 %collective-permute-start.43 = (bf16[144,1024]{1,0:T(8,128)(2,1)S(1)}, bf16[144,1024]{1,0:T(8,128)(2,1)S(1)}, u32[]{:S(2)}, u32[]{:S(2)}) collective-permute-start(bf16[144,1024]{1,0:T(8,128)(2,1)S(1)} %get-tuple-element.93), channel_id=1, source_target_pairs={{0,8},{8,16},{16,24},{24,0},{1,9},{9,17},{17,25},{25,1},{2,10},{10... | collective-permute-start | bytes 884744 | tf_op jit(solution)/shard_map/ppermute | solution.py:44
  265.7 28.7 %collective-permute-start.44 = (bf16[144,1024]{1,0:T(8,128)(2,1)S(1)}, bf16[144,1024]{1,0:T(8,128)(2,1)S(1)}, u32[]{:S(2)}, u32[]{:S(2)}) collective-permute-start(bf16[144,1024]{1,0:T(8,128)(2,1)S(1)} %get-tuple-element.94), channel_id=1, source_target_pairs={{0,12},{4,8},{8,20},{12,16},{16,28},{20,24},{24,4},{28,0},{1,13},{... | collective-permute-start | bytes 884744 | tf_op jit(solution)/shard_map/ppermute | solution.py:51
  269.7 26.9 %collective-permute-start.33 = (bf16[144,1024]{1,0:T(8,128)(2,1)S(1)}, bf16[144,1024]{1,0:T(8,128)(2,1)S(1)}, u32[]{:S(2)}, u32[]{:S(2)}) collective-permute-start(bf16[144,1024]{1,0:T(8,128)(2,1)S(1)} %get-tuple-element.89), channel_id=1, source_target_pairs={{0,16},{8,24},{16,0},{24,8},{1,17},{9,25},{17,1},{25,9},{2,18},{10... | collective-permute-start | bytes 884744 | tf_op jit(solution)/shard_map/ppermute | solution.py:44
  273.4 23.2 %collective-permute-start.34 = (bf16[144,1024]{1,0:T(8,128)(2,1)S(1)}, bf16[144,1024]{1,0:T(8,128)(2,1)S(1)}, u32[]{:S(2)}, u32[]{:S(2)}) collective-permute-start(bf16[144,1024]{1,0:T(8,128)(2,1)S(1)} %get-tuple-element.90), channel_id=1, source_target_pairs={{0,20},{4,16},{8,28},{12,24},{16,4},{20,0},{24,12},{28,8},{1,21},{... | collective-permute-start | bytes 884744 | tf_op jit(solution)/shard_map/ppermute | solution.py:51
  300.8 53.4 %all-to-all-start.1 = ((bf16[8,128,1024]{2,1,0:T(8,128)(2,1)}), bf16[8,128,1024]{2,1,0:T(8,128)(2,1)S(1)}, u32[]{:S(2)}, u32[]{:S(2)}) async-start(bf16[8,128,1024]{2,1,0:T(8,128)(2,1)} %combine2.1), calls=%async_computation.1 | async-start | bytes 4194304 | tf_op jit(solution)/shard_map/all_to_all | solution.py:396
  (30 other events, 470.6 us)
Sparse Core Ops, SparseCore 0:
  9.2 28.8 all-gather.1
